TPU v7x, 32 devices: a whole 2x2x4 slice. The times are simulated.
32 devices in a mesh: chain: 4 (over z), ctx: 4 (over y, x), tp: 2 (over core).
Axes of the slice: x: 2, y: 2, z: 4, core: 2. Of those that a mesh axis runs over, the one named last changes fastest.
Arguments:
- tokens: bfloat16 [16384, 2048], P(('chain', 'ctx')), may hold values from -6 to 6
- w_in: bfloat16 [2048, 3, 2, 1024], P(None, None, 'tp'), may hold values from -0.125 to 0.125
- conv_w: float32 [3, 3, 2, 1024], P(None, None, 'tp'), may hold values from -3 to 3
- w_q: bfloat16 [2048, 256], replicated, may hold values from -0.125 to 0.125
- w_k: bfloat16 [2048, 256], replicated, may hold values from -0.125 to 0.125
- gain: float32 [2, 1024], P('tp'), may hold values from 0.1 to 1.9
- w_o: bfloat16 [2, 1024, 2048], P('tp'), may hold values from -0.125 to 0.125
Outputs:
- out: bfloat16 [16384, 2048], P(('chain', 'ctx', 'tp'))
All inputs are finite; a program needn't handle non-finite values.
Results may differ from a plain program's by a relative error of at most 0.013.
Values may be sent and summed in bfloat16 or wider, within the bound.
No kernel may reach another device: no remote copies, remote signals or barrier semaphores. Data moves between devices by JAX's collectives and lax.ppermute only.
A program may use at most 192 MiB of HBM per device.

v0:
```python
import functools

import jax
import jax.numpy as jnp
from jax import lax
from jax.experimental import pallas as pl
from jax.experimental.pallas import tpu as pltpu
from jax.sharding import PartitionSpec as P

H = 16
F = 16
EPS = 1e-05
CHUNK = 256
GROUPS = 4
PER = H // GROUPS
SLABS = 10
ROWS = SLABS * F
WIDE = SLABS * PER * F
F32 = jnp.float32
BF16 = jnp.bfloat16
MIB = 1 << 20


VM = pl.BlockSpec(memory_space=pltpu.VMEM)
ANY = pl.BlockSpec(memory_space=pl.ANY)
SM = pl.BlockSpec(memory_space=pltpu.SMEM)


def params(mib):
    return pltpu.CompilerParams(vmem_limit_bytes=mib * MIB)


def in_hbm(x):
    return pltpu.with_memory_space_constraint(x, pltpu.HBM)


def columns(src, dst, sems, first, count, at=0):
    return [
        pltpu.make_async_copy(
            src.at[:, (first + j) * 256 : (first + j + 1) * 256],
            dst.at[:, (at + j) * 256 : (at + j + 1) * 256],
            sems.at[j],
        )
        for j in range(count)
    ]


def row_copies(src, dst, sems, count):
    size = dst.shape[0] // count
    return [
        pltpu.make_async_copy(
            src.at[i * size : (i + 1) * size], dst.at[i * size : (i + 1) * size], sems.at[i]
        )
        for i in range(count)
    ]


def dot(a, b):
    return jnp.dot(a, b, preferred_element_type=F32)


def lanes(shape):
    return lax.broadcasted_iota(jnp.int32, shape, len(shape) - 1)


def tile(j, size=256):
    return pl.ds(pl.multiple_of(j * size, size), size)


def qk_body(x, wq, wk, taps, streams, q_out, kt_out, x_out, taps_out, w_out, wqk, sems):
    feats = wq.shape[1]
    w_copies = [
        pltpu.make_async_copy(wq, wqk.at[:, 0:feats], sems.at[0]),
        pltpu.make_async_copy(wk, wqk.at[:, feats : 2 * feats], sems.at[1]),
    ]
    x_copies = row_copies(x, x_out, sems.at[2:6], 4)
    later = columns(streams.at[0], w_out, sems.at[6:8], 0, 2)
    later.append(pltpu.make_async_copy(taps, taps_out, sems.at[8]))
    for copy in w_copies + x_copies + later:
        copy.start()
    for copy in w_copies:
        copy.wait()
    size = x.shape[0] // 4
    for i, copy in enumerate(x_copies):
        copy.wait()
        at = slice(i * size, (i + 1) * size)
        both = dot(x_out[at], wqk[...]).astype(BF16)
        q_out[at] = both[:, :feats]
        kt_out[:, at] = both[:, feats:].astype(F32).T.astype(BF16)
    for copy in later:
        copy.wait()


def project_qk(tokens, w_q, w_k, conv_w, streams):
    rows, width = tokens.shape
    feats = w_q.shape[1]
    return pl.pallas_call(
        qk_body,
        in_specs=[ANY] * 5,
        out_specs=[VM] * 5,
        out_shape=[
            pltpu.VMEM((rows, feats), BF16),
            pltpu.VMEM((feats, rows), BF16),
            pltpu.VMEM((rows, width), BF16),
            pltpu.VMEM(conv_w.shape, F32),
            pltpu.VMEM((width, 512), BF16),
        ],
        scratch_shapes=[pltpu.VMEM((width, 2 * feats), BF16), pltpu.SemaphoreType.DMA((9,))],
        compiler_params=params(16),
        name="project_qk",
    )(in_hbm(tokens), in_hbm(w_q), in_hbm(w_k), in_hbm(conv_w), streams)


def convolve(halo, x, w, taps, stream, j, hold, out):
    rows = x.shape[0]
    at = tile(j)
    hold[0:8] = dot(halo[...], w).astype(BF16).astype(F32)
    for a in range(0, rows, 256):
        hold[8 + a : 264 + a] = dot(x[a : a + 256], w).astype(BF16).astype(F32)
    for a in range(0, rows, 256):
        out[a : a + 256, at] = (
            taps[0, stream, :, at] * hold[8 + a : 264 + a]
            + taps[1, stream, :, at] * hold[7 + a : 263 + a]
            + taps[2, stream, :, at] * hold[6 + a : 262 + a]
        ).astype(BF16)


def key_features(kt, dup, g):
    size = kt.shape[1]
    heads = pl.ds(g * PER, PER)
    own = dup[heads, 0:F]
    slabs = [(own * dup[heads, r : r + F]).astype(BF16) for r in range(8)]
    row = lax.broadcasted_iota(jnp.int32, own.shape, 1)
    last = jnp.where(row < 8, own * dup[heads, 8 : 8 + F], 0.0)
    slabs.append(jnp.where(row == 8, 1.0, last).astype(BF16))
    slabs.append(kt[tile(g, 64)].reshape(PER, F, size))
    return jnp.concatenate([s.reshape(PER * F, size) for s in slabs], axis=0)


def values_body(place, halo_in, x, w_early, streams, taps, kt, v_out, before, halo, w_next, *rest):
    pieces, (hold, dup, flat, w_late, sems) = rest[:-5], rest[-5:]
    n = len(pieces)
    rows = x.shape[0]
    ahead = pltpu.make_async_copy(halo_in, halo, sems.at[6])
    late = columns(streams.at[0], w_late, sems.at[0:2], 2, 2)
    following = row_copies(streams.at[1], w_next, sems.at[2:6], 4)
    for copy in [ahead] + late + following:
        copy.start()
    whole = kt[...].astype(F32).reshape(H, F, rows)
    dup[:, 0:F] = whole
    dup[:, F : 2 * F] = whole
    low = lanes((SLABS, F, 128)) < 64
    ahead.wait()

    def group(w_ref, first, j, carry):
        g = first + j
        convolve(halo, x, w_ref[:, tile(j)], taps, 0, g, hold, v_out)
        feats = key_features(kt, dup, g)
        left = right = jnp.zeros((ROWS, 128), F32)
        for c in range(rows // CHUNK):
            at = slice(c * CHUNK, (c + 1) * CHUNK)
            before[c, g, :, :128] = left.astype(BF16)
            before[c, g, :, 128:] = right.astype(BF16)
            state = dot(feats[:, at], v_out[at, tile(g)])
            state = state.reshape(SLABS, PER, F, 256)
            left += jnp.where(low, state[:, 0, :, :128], state[:, 1, :, :128]).reshape(ROWS, 128)
            right += jnp.where(low, state[:, 2, :, 128:], state[:, 3, :, 128:]).reshape(ROWS, 128)
        flat[g, :, :128] = left.astype(BF16)
        flat[g, :, 128:] = right.astype(BF16)
        return carry

    lax.fori_loop(0, 2, functools.partial(group, w_early, 0), 0)
    for copy in late:
        copy.wait()
    lax.fori_loop(0, 2, functools.partial(group, w_late, 2), 0)
    split = flat.reshape(n, GROUPS * ROWS // n, 256)
    for m, piece in enumerate(pieces):
        piece[...] = split[lax.rem(place[0] + m, n)]
    for copy in following:
        copy.wait()


def project_values(place, halo, x, w_early, streams, taps, kt, n):
    rows, width = x.shape
    half = streams.shape[2]
    part = GROUPS * ROWS // n
    return pl.pallas_call(
        values_body,
        in_specs=[SM, ANY, VM, VM, ANY, VM, VM],
        out_specs=[VM] * (4 + n),
        out_shape=[
            pltpu.VMEM((rows, half), BF16),
            pltpu.VMEM((rows // CHUNK, GROUPS, ROWS, 256), BF16),
            pltpu.VMEM(halo.shape, BF16),
            pltpu.VMEM((width, half), BF16),
        ]
        + [jax.ShapeDtypeStruct((part, 256), BF16) for _ in range(n)],
        scratch_shapes=[
            pltpu.VMEM((rows + 8, 256), F32),
            pltpu.VMEM((H, 2 * F, rows), F32),
            pltpu.VMEM((GROUPS, ROWS, 256), BF16),
            pltpu.VMEM((width, 512), BF16),
            pltpu.SemaphoreType.DMA((7,)),
        ],
        compiler_params=params(20),
        name="project_values",
    )(place, halo, x, w_early, streams, taps, kt)


def gate_body(halo, x, w, taps, streams, out, w_next, hold, sems):
    copies = row_copies(streams.at[2], w_next, sems, 4)
    for copy in copies:
        copy.start()

    def step(j, carry):
        convolve(halo, x, w[:, tile(j)], taps, 1, j, hold, out)
        return carry

    lax.fori_loop(0, w.shape[1] // 256, step, 0)
    for copy in copies:
        copy.wait()


def project_gate(halo, x, w, taps, streams):
    rows = x.shape[0]
    return pl.pallas_call(
        gate_body,
        in_specs=[VM, VM, VM, VM, ANY],
        out_specs=[VM] * 2,
        out_shape=[pltpu.VMEM((rows, w.shape[1]), BF16), pltpu.VMEM(w.shape, BF16)],
        scratch_shapes=[pltpu.VMEM((rows + 8, 256), F32), pltpu.SemaphoreType.DMA((4,))],
        compiler_params=params(16),
        name="project_gate",
    )(halo, x, w, taps, streams)


def skip_body(halo, x, w, taps, w_o, gain, out, w_next, gain_out, choose, hold, sems):
    copies = row_copies(w_o, w_next, sems.at[0:4], 4)
    copies.append(pltpu.make_async_copy(gain, gain_out, sems.at[4]))
    for copy in copies:
        copy.start()
    for parity in range(2):
        choose[parity] = selection(parity)

    def step(j, carry):
        convolve(halo, x, w[:, tile(j)], taps, 2, j, hold, out)
        return carry

    lax.fori_loop(0, w.shape[1] // 256, step, 0)
    for copy in copies:
        copy.wait()


def project_skip(halo, x, w, taps, w_o, gain):
    rows = x.shape[0]
    return pl.pallas_call(
        skip_body,
        in_specs=[VM, VM, VM, VM, ANY, ANY],
        out_specs=[VM] * 4,
        out_shape=[
            pltpu.VMEM((rows, w.shape[1]), BF16),
            pltpu.VMEM(w_o.shape, BF16),
            pltpu.VMEM(gain.shape, F32),
            pltpu.VMEM((2, 128, WIDE + 128), BF16),
        ],
        scratch_shapes=[pltpu.VMEM((rows + 8, 256), F32), pltpu.SemaphoreType.DMA((5,))],
        compiler_params=params(16),
        name="project_skip",
    )(halo, x, w, taps, w_o, gain)


def total_body(*refs):
    found = refs[0][...].astype(F32)
    for part in refs[1:-1]:
        found += part[...].astype(F32)
    refs[-1][...] = found.astype(BF16)


def add_up(parts):
    return pl.pallas_call(
        total_body,
        in_specs=[VM] * len(parts),
        out_specs=VM,
        out_shape=jax.ShapeDtypeStruct(parts[0].shape, BF16),
        compiler_params=params(8),
        name="add_up",
    )(*parts)


def starts_body(n, place, *refs):
    parts, earlier, outs, hold = refs[:n], refs[n : -n - 1], refs[-n - 1 : -1], refs[-1]
    for k, part in enumerate(parts):
        hold[lax.rem(place[0] + n - k, n)] = part[...].astype(F32)
    found = jnp.zeros(parts[0].shape, F32)
    for d, block in enumerate(earlier):
        found += jnp.where(place[3] > d, block[...].astype(F32), 0.0)
    for p in range(n):
        own = hold[p]
        hold[p] = found
        found += own
    for m, out in enumerate(outs):
        out[...] = hold[lax.rem(place[0] + m, n)].astype(BF16)


def start_states(place, parts, earlier):
    n, shape = len(parts), parts[0].shape
    return pl.pallas_call(
        functools.partial(starts_body, n),
        in_specs=[SM] + [VM] * (n + len(earlier)),
        out_specs=[VM] * n,
        out_shape=[jax.ShapeDtypeStruct(shape, BF16) for _ in range(n)],
        scratch_shapes=[pltpu.VMEM((n,) + shape, F32)],
        compiler_params=params(8),
        name="start_states",
    )(place, *parts, *earlier)


def inside_body(after, q, kt, v, out):
    low = lanes((CHUNK, 128)) < 64
    head = lanes((CHUNK, 128)) // F
    causal = lax.broadcasted_iota(jnp.int32, (CHUNK, CHUNK), 0) >= lanes((CHUNK, CHUNK))

    def chunk(c, carry):
        rows = tile(c, CHUNK)
        for part in range(2):
            query = q[rows, part * 128 : (part + 1) * 128] * 0.25
            stacked = jnp.concatenate(
                [jnp.where(head == h, query, 0.0).astype(BF16) for h in range(8)], axis=0
            )
            score = dot(stacked, kt[part * 128 : (part + 1) * 128, rows])
            for pair in range(4):
                both = []
                at = part * 512 + pair * 128
                for h in (2 * pair, 2 * pair + 1):
                    x = score[h * CHUNK : (h + 1) * CHUNK]
                    poly = x * (0.5 * x + 1.0) + 1.0
                    weight = jnp.where(causal, poly, 0.0).astype(BF16)
                    both.append(dot(weight, v[rows, at : at + 128]))
                out[rows, at : at + 128] = jnp.where(low, both[0], both[1])
        return carry

    lax.fori_loop(0, q.shape[0] // CHUNK, chunk, 0)


def inside(after, q, kt, v):
    return pl.pallas_call(
        inside_body,
        in_specs=[ANY, VM, VM, VM],
        out_specs=VM,
        out_shape=pltpu.VMEM(v.shape, F32),
        compiler_params=params(16),
        name="inside",
    )(after, q, kt, v)


def selection(parity):
    shape = (128, WIDE + 128)
    src = lax.broadcasted_iota(jnp.int32, shape, 0)
    col = lanes(shape)
    slab, h, i = col // 64, (col // F) % PER, col % F
    turn_by = jnp.where(slab < 9, slab, 0)
    want = parity * 64 + h * F + (i + turn_by) % F
    scale = jnp.where(slab == 0, 1.0 / 32, jnp.where(slab < 9, 1.0 / 16, 0.25))
    scale = jnp.where(slab > 9, 1.0, scale)
    scale = jnp.where((slab == 8) & (i >= 8), 0.0, scale)
    return jnp.where(src == want, scale, 0.0).astype(BF16)


def mix(start, base, c, q, att, before, gate, skip, gain, choose, mixed):
    rows = tile(base + c, CHUNK)
    lane = lanes((CHUNK, 128))
    one = jnp.where((lane < 64) & (lane % F == 8), 1.0, 0.0)
    wide = lanes((SLABS, F, 256)) // 64
    mean = lax.broadcasted_iota(jnp.int32, (256, 256), 0) // 64 == lanes((256, 256)) // 64
    mean = jnp.where(mean, 1.0 / 64, 0.0).astype(BF16)
    for g in range(GROUPS):
        query = q[rows, g // 2 * 128 : g // 2 * 128 + 128]
        b = dot(query, choose[g % 2])
        a = b[:, WIDE:]
        feats = [(a * b[:, s * 128 : (s + 1) * 128]).astype(BF16) for s in range(4)]
        b4 = b[:, 512:640]
        feats.append((jnp.where(lane < 64, a * b4, b4) + one).astype(BF16))
        state = (start[g].astype(F32) + before[base + c, g].astype(F32)).astype(BF16)
        state = state.reshape(SLABS, F, 256)
        state = jnp.stack([jnp.where(wide == h, state, 0.0).astype(BF16) for h in range(PER)], axis=1)
        at = slice(g * 256, (g + 1) * 256)
        whole = att[rows, at] + dot(jnp.concatenate(feats, axis=1), state.reshape(WIDE, 256))
        mean_sq = dot((whole * whole).astype(BF16), mean)
        normed = (whole * lax.rsqrt(mean_sq + EPS)).astype(BF16).astype(F32)
        gates = gate[rows, at].astype(F32)
        act = 0.5 * gates * (1.0 + jnp.tanh(0.5 * gates))
        made = act * (normed * gain[:, at] + skip[rows, at].astype(F32))
        mixed[tile(c, CHUNK), at] = made.astype(BF16)


def gather_start(place, pieces, start):
    n = len(pieces)
    split = start.reshape(n, GROUPS * ROWS // n, 256)
    for m, piece in enumerate(pieces):
        split[lax.rem(place[0] + n - m, n)] = piece[...]


def away_body(place, q, att, before, gate, skip, gain, choose, w_o, *rest):
    pieces, (out, start, mixed) = rest[:-3], rest[-3:]
    gather_start(place, pieces, start)

    def chunk(c, carry):
        mix(start, place[1], c, q, att, before, gate, skip, gain, choose, mixed)
        return carry

    lax.fori_loop(0, out.shape[0] // CHUNK, chunk, 0)

    def columns_of(j, carry):
        out[:, tile(j, 512)] = dot(mixed[...], w_o[:, tile(j, 512)]).astype(BF16)
        return carry

    lax.fori_loop(0, out.shape[1] // 512, columns_of, 0)


def home_body(place, after, q, att, before, gate, skip, gain, choose, *rest):
    pieces, (mixed, start) = rest[:-2], rest[-2:]
    gather_start(place, pieces, start)

    def chunk(c, carry):
        mix(start, place[2], c, q, att, before, gate, skip, gain, choose, mixed)
        return carry

    lax.fori_loop(0, mixed.shape[0] // CHUNK, chunk, 0)


def away(place, tail, w_o, pieces, rows):
    half, width = w_o.shape
    return pl.pallas_call(
        away_body,
        in_specs=[SM] + [VM] * (len(tail) + 1 + len(pieces)),
        out_specs=VM,
        out_shape=jax.ShapeDtypeStruct((rows, width), BF16),
        scratch_shapes=[pltpu.VMEM((GROUPS, ROWS, 256), BF16), pltpu.VMEM((rows, half), BF16)],
        compiler_params=params(16),
        name="away",
    )(place, *tail, w_o, *pieces)


def home(place, after, tail, pieces, rows, half):
    return pl.pallas_call(
        home_body,
        in_specs=[SM, ANY] + [VM] * (len(tail) + len(pieces)),
        out_specs=VM,
        out_shape=pltpu.VMEM((rows, half), BF16),
        scratch_shapes=[pltpu.VMEM((GROUPS, ROWS, 256), BF16)],
        compiler_params=params(16),
        name="home",
    )(place, after, *tail, *pieces)


def join_body(mixed, w_o, other, out, hold, sems):
    copies = []
    for j in range(out.shape[1] // 512):
        at = slice(j * 512, (j + 1) * 512)
        own = dot(mixed[...], w_o[:, at]).astype(BF16).astype(F32)
        hold[:, at] = (own + other[:, at].astype(F32)).astype(BF16)
        copies.append(pltpu.make_async_copy(hold.at[:, at], out.at[:, at], sems.at[j]))
        copies[-1].start()
    for copy in copies:
        copy.wait()


def join(mixed, w_o, other):
    return pl.pallas_call(
        join_body,
        in_specs=[VM, VM, VM],
        out_specs=pl.BlockSpec(memory_space=pltpu.HBM),
        out_shape=jax.ShapeDtypeStruct(other.shape, BF16),
        scratch_shapes=[
            pltpu.VMEM(other.shape, BF16),
            pltpu.SemaphoreType.DMA((other.shape[1] // 512,)),
        ],
        compiler_params=params(16),
        name="join",
    )(mixed, w_o, other)


def shift(block, axes, distance, size):
    return lax.ppermute(block, axes, [(i, i + distance) for i in range(size - distance)])


def turn(block, axis, distance, size):
    return lax.ppermute(block, axis, [(i, (i + distance) % size) for i in range(size)])


def per_device(tokens, w_in, conv_w, w_q, w_k, gain, w_o):
    rows, width = tokens.shape
    half = w_in.shape[3]
    n, blocks = lax.axis_size("ctx"), lax.axis_size("chain")
    me, core = lax.axis_index("ctx"), lax.axis_index("tp")
    per_half = rows // CHUNK // 2
    block = lax.axis_index("chain")
    place = jnp.stack([me, (1 - core) * per_half, core * per_half, block]).astype(jnp.int32)
    streams = in_hbm(w_in.transpose(1, 2, 0, 3).reshape(3, width, half))
    w_out = in_hbm(w_o.reshape(half, width))

    halo = shift(tokens[rows - 8 :], ("chain", "ctx"), 1, n * blocks)
    q, kt, x, taps, w_early = project_qk(tokens, w_q, w_k, conv_w, streams)
    values, before, halo, w_gate, *mine = project_values(
        place, in_hbm(halo), x, w_early, streams, taps, kt, n
    )
    theirs = [mine[0]] + [turn(mine[m], "ctx", m, n) for m in range(1, n)]
    gate, w_skip = project_gate(halo, x, w_gate, taps, streams)
    theirs, gate = lax.optimization_barrier((theirs, gate))
    total = add_up(theirs)
    earlier = [turn(total, "chain", d, blocks) for d in range(1, blocks)]
    skip, weight, gains, choose = project_skip(halo, x, w_skip, taps, w_out, in_hbm(gain))
    earlier, skip = lax.optimization_barrier((earlier, skip))
    starts = start_states(place, theirs, earlier)
    got = [starts[0]] + [turn(starts[m], "ctx", m, n) for m in range(1, n)]
    att = inside(starts[0], q, kt, values)
    got, att = lax.optimization_barrier((got, att))
    tail = (q, att, before, gate, skip, gains, choose)
    sent = away(place, tail, weight, got, rows // 2)
    swapped = lax.ppermute(sent, "tp", [(0, 1), (1, 0)])
    mixed = home(place, sent, tail, got, rows // 2, half)
    return join(mixed, weight, swapped)


def solution(mesh):
    return jax.shard_map(
        per_device,
        mesh=mesh,
        in_specs=(
            P(("chain", "ctx"), None),
            P(None, None, "tp", None),
            P(None, None, "tp", None),
            P(),
            P(),
            P("tp", None),
            P("tp", None, None),
        ),
        out_specs=P(("chain", "ctx", "tp"), None),
        check_vma=False,
    )
```

profile of v0, /device:TPU:1, one launch (start us, length us, event | category | flops | bytes accessed | tf_op | source)
XLA Modules:
  0.0 70.7 jit_solution(17977768932204234422)
XLA Ops:
  0.0 0.8 %slice.3 = bf16[8,2048]{1,0:T(8,128)(2,1)S(1)} slice(bf16[1024,2048]{1,0:T(8,128)(2,1)} %x.1), slice={[1016:1024], [0:2048]} | slice | bytes 65536 | tf_op jit(solution)/shard_map/slice | solution.py:502
  0.8 3.9 %collective-permute-start = (bf16[8,2048]{1,0:T(8,128)(2,1)S(1)}, bf16[8,2048]{1,0:T(8,128)(2,1)S(1)}, u32[]{:S(2)}, u32[]{:S(2)}) collective-permute-start(bf16[8,2048]{1,0:T(8,128)(2,1)S(1)} %slice.3), channel_id=1, source_target_pairs={{0,2},{2,4},{4,6},{6,8},{8,10},{10,12},{12,14},{14,16},{16,18},{18... | collective-permute-start | bytes 98312 | tf_op jit(solution)/shard_map/ppermute | solution.py:484
  4.7 0.1 pad_add_fusion.place
  4.8 5.1 %project_qk.1 = (bf16[1024,256]{1,0:T(8,128)(2,1)S(1)}, bf16[256,1024]{1,0:T(8,128)(2,1)S(1)}, bf16[1024,2048]{1,0:T(8,128)(2,1)S(1)}, f32[3,3,1,1024]{3,2,1,0:T(1,128)S(1)}, bf16[2048,512]{1,0:T(8,128)(2,1)S(1)}) custom-call(bf16[1024,2048]{1,0:T(8,128)(2,1)} %x.1, bf16[2048,256]{1,0:T(8,128)(2,1)} %wq.1, bf16[2048,256]{1,0:T(8,128)(2,1)} %wk.1, ...), custom_call_target="tpu_custom_call" | custom-call | tf_op jit(solution)/shard_map/project_qk/pallas_call | solution.py:97
  9.8 0.0 collective-permute-done.halo_in
  9.9 0.0 copy-start
  9.9 0.6 copy-done
  10.5 9.9 %project_values.1 = (bf16[1024,1024]{1,0:T(8,128)(2,1)S(1)}, bf16[4,4,160,256]{3,2,1,0:T(8,128)(2,1)S(1)}, bf16[8,2048]{1,0:T(8,128)(2,1)S(1)}, bf16[2048,1024]{...) custom-call(s32[4]{0:T(128)S(1)} %pad_add_fusion.place, ...), custom_call_target="tpu_custom_call" | custom-call | tf_op jit(solution)/shard_map/project_values/pallas_call | solution.py:187
  20.4 1.3 %collective-permute-start.1 = (bf16[160,256]{1,0:T(8,128)(2,1)S(1)}, bf16[160,256]{1,0:T(8,128)(2,1)S(1)}, u32[]{:S(2)}, u32[]{:S(2)}) collective-permute-start(bf16[160,256]{1,0:T(8,128)(2,1)S(1)} %get-tuple-element.48), channel_id=1, source_target_pairs={{0,2},{2,4},{4,6},{6,0},{1,3},{3,5},{5,7},{7,1},{8,10},{10,12},{12... | collective-permute-start | bytes 245768 | tf_op jit(solution)/shard_map/ppermute | solution.py:488
  21.7 1.2 %collective-permute-start.2 = (bf16[160,256]{1,0:T(8,128)(2,1)S(1)}, bf16[160,256]{1,0:T(8,128)(2,1)S(1)}, u32[]{:S(2)}, u32[]{:S(2)}) collective-permute-start(bf16[160,256]{1,0:T(8,128)(2,1)S(1)} %get-tuple-element.49), channel_id=1, source_target_pairs={{0,4},{2,6},{4,0},{6,2},{1,5},{3,7},{5,1},{7,3},{8,12},{10,14},{12... | collective-permute-start | bytes 245768 | tf_op jit(solution)/shard_map/ppermute | solution.py:488
  22.9 1.2 %collective-permute-start.3 = (bf16[160,256]{1,0:T(8,128)(2,1)S(1)}, bf16[160,256]{1,0:T(8,128)(2,1)S(1)}, u32[]{:S(2)}, u32[]{:S(2)}) collective-permute-start(bf16[160,256]{1,0:T(8,128)(2,1)S(1)} %get-tuple-element.50), channel_id=1, source_target_pairs={{0,6},{2,0},{4,2},{6,4},{1,7},{3,1},{5,3},{7,5},{8,14},{10,8},{12,... | collective-permute-start | bytes 245768 | tf_op jit(solution)/shard_map/ppermute | solution.py:488
  24.1 6.6 %project_gate.1 = (bf16[1024,1024]{1,0:T(8,128)(2,1)S(1)}, bf16[2048,1024]{1,0:T(8,128)(2,1)S(1)}) custom-call(bf16[8,2048]{1,0:T(8,128)(2,1)S(1)} %get-tuple-element.51.halo, bf16[1024,2048]{1,0:T(8,128)(2,1)S(1)} %get-tuple-element.43.x, bf16[2048,1024]{1,0:T(8,128)(2,1)S(1)} %get-tuple-element.52.w, f32[3,3,1,1024]{3,2,1,0:T(1,128)S(1)} %get-tuple-element.45.taps, ...), custom_call_target="tpu_custom_call" | custom-call | tf_op jit(solution)/shard_map/project_gate/pallas_call | solution.py:226
  30.7 0.0 collective-permute-done.1.refs_1_
  30.7 0.0 collective-permute-done.2.refs_2_
  30.7 0.0 collective-permute-done.3.refs_3_
  30.8 1.4 %collective-permute-start.4 = (bf16[160,256]{1,0:T(8,128)(2,1)S(1)}, bf16[160,256]{1,0:T(8,128)(2,1)S(1)}, u32[]{:S(2)}, u32[]{:S(2)}) collective-permute-start(bf16[160,256]{1,0:T(8,128)(2,1)S(1)} %add_up.1), channel_id=1, source_target_pairs={{0,8},{8,16},{16,24},{24,0},{1,9},{9,17},{17,25},{25,1},{2,10},{10... | collective-permute-start | bytes 245768 | tf_op jit(solution)/shard_map/ppermute | solution.py:488
  32.1 2.3 %collective-permute-start.5 = (bf16[160,256]{1,0:T(8,128)(2,1)S(1)}, bf16[160,256]{1,0:T(8,128)(2,1)S(1)}, u32[]{:S(2)}, u32[]{:S(2)}) collective-permute-start(bf16[160,256]{1,0:T(8,128)(2,1)S(1)} %add_up.1), channel_id=1, source_target_pairs={{0,16},{8,24},{16,0},{24,8},{1,17},{9,25},{17,1},{25,9},{2,18},{10... | collective-permute-start | bytes 245768 | tf_op jit(solution)/shard_map/ppermute | solution.py:488
  34.4 1.1 %collective-permute-start.6 = (bf16[160,256]{1,0:T(8,128)(2,1)S(1)}, bf16[160,256]{1,0:T(8,128)(2,1)S(1)}, u32[]{:S(2)}, u32[]{:S(2)}) collective-permute-start(bf16[160,256]{1,0:T(8,128)(2,1)S(1)} %add_up.1), channel_id=1, source_target_pairs={{0,24},{8,0},{16,8},{24,16},{1,25},{9,1},{17,9},{25,17},{2,26},{10... | collective-permute-start | bytes 245768 | tf_op jit(solution)/shard_map/ppermute | solution.py:488
  35.5 6.7 %project_skip.1 = (bf16[1024,1024]{1,0:T(8,128)(2,1)S(1)}, bf16[1024,2048]{1,0:T(8,128)(2,1)S(1)}, f32[1,1024]{1,0:T(1,128)S(1)}, bf16[2,128,768]{2,1,0:T(8,128)(2,1)S(1)}) custom-call(bf16[8,2048]{1,0:T(8,128)(2,1)S(1)} %get-tuple-element.51.halo, bf16[1024,2048]{1,0:T(8,128)(2,1)S(1)} %get-tuple-element.43.x, bf16[2048,1024]{1,0:T(8,128)(2,1)S(1)} %get-tuple-element.58.w, ...), custom_call_target="tpu_custom_call" | custom-call | tf_op jit(solution)/shard_map/project_skip/pallas_call | solution.py:256
  42.2 0.0 collective-permute-done.4.refs_4_
  42.2 0.0 collective-permute-done.5.refs_5_
  42.2 0.0 collective-permute-done.6.refs_6_
  42.3 0.7 %start_states.1 = (bf16[160,256]{1,0:T(8,128)(2,1)S(1)}, bf16[160,256]{1,0:T(8,128)(2,1)S(1)}, bf16[160,256]{1,0:T(8,128)(2,1)S(1)}, bf16[160,256]{1,0:T(8,128)(2,1)S(1)}) custom-call(s32[4]{0:T(128)S(1)} %pad_add_fusion.place, bf16[160,256]{1,0:T(8,128)(2,1)S(1)} %get-tuple-element.54.refs_0_, bf16[160,256]{1,0:T(8,128)(2,1)S(1)} %collective-permute-done.1.refs_1_, ...), custom_call_target="tpu_custom_call" | custom-call | tf_op jit(solution)/shard_map/start_states/pallas_call | solution.py:307
  43.0 0.4 collective-permute-start.7
  43.3 0.2 collective-permute-start.8
  43.6 2.0 %collective-permute-start.9 = (bf16[160,256]{1,0:T(8,128)(2,1)S(1)}, bf16[160,256]{1,0:T(8,128)(2,1)S(1)}, u32[]{:S(2)}, u32[]{:S(2)}) collective-permute-start(bf16[160,256]{1,0:T(8,128)(2,1)S(1)} %get-tuple-element.66), channel_id=1, source_target_pairs={{0,6},{2,0},{4,2},{6,4},{1,7},{3,1},{5,3},{7,5},{8,14},{10,8},{12,... | collective-permute-start | bytes 245768 | tf_op jit(solution)/shard_map/ppermute | solution.py:488
  45.6 5.4 %inside.1.att = f32[1024,1024]{1,0:T(8,128)S(1)} custom-call(bf16[160,256]{1,0:T(8,128)(2,1)S(1)} %get-tuple-element.75.after.rest_0_, bf16[1024,256]{1,0:T(8,128)(2,1)S(1)} %get-tuple-element.42.q, bf16[256,1024]{1,0:T(8,128)(2,1)S(1)} %get-tuple-element.46.kt, bf16[1024,1024]{1,0:T(8,128)(2,1)S(1)} %get-tuple-element.67.v), custom_call_target="tpu_custom_call" | custom-call | tf_op jit(solution)/shard_map/inside/pallas_call | solution.py:346
  51.1 0.0 collective-permute-done.7.rest_1_
  51.1 0.0 collective-permute-done.8.rest_2_
  51.1 0.0 collective-permute-done.9.rest_3_
  51.1 7.7 %away.1.after = bf16[512,2048]{1,0:T(8,128)(2,1)S(1)} custom-call(s32[4]{0:T(128)S(1)} %pad_add_fusion.place, bf16[1024,256]{1,0:T(8,128)(2,1)S(1)} %get-tuple-element.42.q, f32[1024,1024]{1,0:T(8,128)S(1)} %inside.1.att, bf16[4,4,160,256]{3,2,1,0:T(8,128)(2,1)S(1)} %get-tuple-element.69.before, bf16[1024,1024]{1,0:T(8,128)(2,1)S(1)} %get-tuple-element.70.gate, ...), custom_call_target="tpu_custom_call" | custom-call | tf_op jit(solution)/shard_map/away/pallas_call | solution.py:433
  58.8 3.5 %collective-permute-start.10 = (bf16[512,2048]{1,0:T(8,128)(2,1)S(1)}, bf16[512,2048]{1,0:T(8,128)(2,1)S(1)}, u32[]{:S(2)}, u32[]{:S(2)}) collective-permute-start(bf16[512,2048]{1,0:T(8,128)(2,1)S(1)} %away.1.after), channel_id=1, source_target_pairs={{0,1},{1,0},{2,3},{3,2},{4,5},{5,4},{6,7},{7,6},{8,9},{9,8},{10,11... | collective-permute-start | bytes 6291464 | tf_op jit(solution)/shard_map/ppermute | solution.py:520
  62.4 4.9 %home.1.mixed = bf16[512,1024]{1,0:T(8,128)(2,1)S(1)} custom-call(s32[4]{0:T(128)S(1)} %pad_add_fusion.place, bf16[512,2048]{1,0:T(8,128)(2,1)S(1)} %away.1.after, bf16[1024,256]{1,0:T(8,128)(2,1)S(1)} %get-tuple-element.42.q, f32[1024,1024]{1,0:T(8,128)S(1)} %inside.1.att, bf16[4,4,160,256]{3,2,1,0:T(8,128)(2,1)S(1)} %get-tuple-element.69.before, ...), custom_call_target="tpu_custom_call" | custom-call | tf_op jit(solution)/shard_map/home/pallas_call | solution.py:445
  67.3 0.0 collective-permute-done.10.other
  67.3 3.3 %join.1 = bf16[512,2048]{1,0:T(8,128)(2,1)} custom-call(bf16[512,1024]{1,0:T(8,128)(2,1)S(1)} %home.1.mixed, bf16[1024,2048]{1,0:T(8,128)(2,1)S(1)} %get-tuple-element.74.w_o, bf16[512,2048]{1,0:T(8,128)(2,1)S(1)} %collective-permute-done.10.other), custom_call_target="tpu_custom_call" | custom-call | tf_op jit(solution)/shard_map/join/pallas_call | solution.py:469
  (1 shorter events, 0.0 us)
Async XLA Ops:
  0.8 9.1 %collective-permute-start = (bf16[8,2048]{1,0:T(8,128)(2,1)S(1)}, bf16[8,2048]{1,0:T(8,128)(2,1)S(1)}, u32[]{:S(2)}, u32[]{:S(2)}) collective-permute-start(bf16[8,2048]{1,0:T(8,128)(2,1)S(1)} %slice.3), channel_id=1, source_target_pairs={{0,2},{2,4},{4,6},{6,8},{8,10},{10,12},{12,14},{14,16},{16,18},{18... | collective-permute-start | bytes 98312 | tf_op jit(solution)/shard_map/ppermute | solution.py:484
  9.9 0.6 copy-start
  20.4 10.3 %collective-permute-start.1 = (bf16[160,256]{1,0:T(8,128)(2,1)S(1)}, bf16[160,256]{1,0:T(8,128)(2,1)S(1)}, u32[]{:S(2)}, u32[]{:S(2)}) collective-permute-start(bf16[160,256]{1,0:T(8,128)(2,1)S(1)} %get-tuple-element.48), channel_id=1, source_target_pairs={{0,2},{2,4},{4,6},{6,0},{1,3},{3,5},{5,7},{7,1},{8,10},{10,12},{12... | collective-permute-start | bytes 245768 | tf_op jit(solution)/shard_map/ppermute | solution.py:488
  21.7 9.0 %collective-permute-start.2 = (bf16[160,256]{1,0:T(8,128)(2,1)S(1)}, bf16[160,256]{1,0:T(8,128)(2,1)S(1)}, u32[]{:S(2)}, u32[]{:S(2)}) collective-permute-start(bf16[160,256]{1,0:T(8,128)(2,1)S(1)} %get-tuple-element.49), channel_id=1, source_target_pairs={{0,4},{2,6},{4,0},{6,2},{1,5},{3,7},{5,1},{7,3},{8,12},{10,14},{12... | collective-permute-start | bytes 245768 | tf_op jit(solution)/shard_map/ppermute | solution.py:488
  22.9 7.8 %collective-permute-start.3 = (bf16[160,256]{1,0:T(8,128)(2,1)S(1)}, bf16[160,256]{1,0:T(8,128)(2,1)S(1)}, u32[]{:S(2)}, u32[]{:S(2)}) collective-permute-start(bf16[160,256]{1,0:T(8,128)(2,1)S(1)} %get-tuple-element.50), channel_id=1, source_target_pairs={{0,6},{2,0},{4,2},{6,4},{1,7},{3,1},{5,3},{7,5},{8,14},{10,8},{12,... | collective-permute-start | bytes 245768 | tf_op jit(solution)/shard_map/ppermute | solution.py:488
  30.8 11.5 %collective-permute-start.4 = (bf16[160,256]{1,0:T(8,128)(2,1)S(1)}, bf16[160,256]{1,0:T(8,128)(2,1)S(1)}, u32[]{:S(2)}, u32[]{:S(2)}) collective-permute-start(bf16[160,256]{1,0:T(8,128)(2,1)S(1)} %add_up.1), channel_id=1, source_target_pairs={{0,8},{8,16},{16,24},{24,0},{1,9},{9,17},{17,25},{25,1},{2,10},{10... | collective-permute-start | bytes 245768 | tf_op jit(solution)/shard_map/ppermute | solution.py:488
  32.1 10.1 %collective-permute-start.5 = (bf16[160,256]{1,0:T(8,128)(2,1)S(1)}, bf16[160,256]{1,0:T(8,128)(2,1)S(1)}, u32[]{:S(2)}, u32[]{:S(2)}) collective-permute-start(bf16[160,256]{1,0:T(8,128)(2,1)S(1)} %add_up.1), channel_id=1, source_target_pairs={{0,16},{8,24},{16,0},{24,8},{1,17},{9,25},{17,1},{25,9},{2,18},{10... | collective-permute-start | bytes 245768 | tf_op jit(solution)/shard_map/ppermute | solution.py:488
  34.4 7.8 %collective-permute-start.6 = (bf16[160,256]{1,0:T(8,128)(2,1)S(1)}, bf16[160,256]{1,0:T(8,128)(2,1)S(1)}, u32[]{:S(2)}, u32[]{:S(2)}) collective-permute-start(bf16[160,256]{1,0:T(8,128)(2,1)S(1)} %add_up.1), channel_id=1, source_target_pairs={{0,24},{8,0},{16,8},{24,16},{1,25},{9,1},{17,9},{25,17},{2,26},{10... | collective-permute-start | bytes 245768 | tf_op jit(solution)/shard_map/ppermute | solution.py:488
  43.0 8.1 %collective-permute-start.7 = (bf16[160,256]{1,0:T(8,128)(2,1)S(1)}, bf16[160,256]{1,0:T(8,128)(2,1)S(1)}, u32[]{:S(2)}, u32[]{:S(2)}) collective-permute-start(bf16[160,256]{1,0:T(8,128)(2,1)S(1)} %get-tuple-element.64), channel_id=1, source_target_pairs={{0,2},{2,4},{4,6},{6,0},{1,3},{3,5},{5,7},{7,1},{8,10},{10,12},{12... | collective-permute-start | bytes 245768 | tf_op jit(solution)/shard_map/ppermute | solution.py:488
  43.3 7.8 %collective-permute-start.8 = (bf16[160,256]{1,0:T(8,128)(2,1)S(1)}, bf16[160,256]{1,0:T(8,128)(2,1)S(1)}, u32[]{:S(2)}, u32[]{:S(2)}) collective-permute-start(bf16[160,256]{1,0:T(8,128)(2,1)S(1)} %get-tuple-element.65), channel_id=1, source_target_pairs={{0,4},{2,6},{4,0},{6,2},{1,5},{3,7},{5,1},{7,3},{8,12},{10,14},{12... | collective-permute-start | bytes 245768 | tf_op jit(solution)/shard_map/ppermute | solution.py:488
  43.6 7.5 %collective-permute-start.9 = (bf16[160,256]{1,0:T(8,128)(2,1)S(1)}, bf16[160,256]{1,0:T(8,128)(2,1)S(1)}, u32[]{:S(2)}, u32[]{:S(2)}) collective-permute-start(bf16[160,256]{1,0:T(8,128)(2,1)S(1)} %get-tuple-element.66), channel_id=1, source_target_pairs={{0,6},{2,0},{4,2},{6,4},{1,7},{3,1},{5,3},{7,5},{8,14},{10,8},{12,... | collective-permute-start | bytes 245768 | tf_op jit(solution)/shard_map/ppermute | solution.py:488
  58.8 8.4 %collective-permute-start.10 = (bf16[512,2048]{1,0:T(8,128)(2,1)S(1)}, bf16[512,2048]{1,0:T(8,128)(2,1)S(1)}, u32[]{:S(2)}, u32[]{:S(2)}) collective-permute-start(bf16[512,2048]{1,0:T(8,128)(2,1)S(1)} %away.1.after), channel_id=1, source_target_pairs={{0,1},{1,0},{2,3},{3,2},{4,5},{5,4},{6,7},{7,6},{8,9},{9,8},{10,11... | collective-permute-start | bytes 6291464 | tf_op jit(solution)/shard_map/ppermute | solution.py:520
where the time goes:
time: 70.9 us; the launch traced here: 70.7 us
  Pallas kernels  50.4 us (71%)
  starting transfers between devices  18.5 us (26%)
  local copies, waits for them, and re-layouts  1.37 us (2%)
    ppermute x9, starting transfers between devices, turn(): lax.ppermute(block, axis, [(i, (i + distance) % size) for i in range(size)])  11 us
    pallas_call x1, Pallas kernels, project_values(): pl.pallas_call(values_body, in_specs=[SM, ANY, VM, VM, ANY, VM, VM], out_...  9.91 us
    pallas_call x1, Pallas kernels, away(): pl.pallas_call(away_body, in_specs=[SM] + [VM] * (len(tail) + 1 + len(pie...  7.72 us
    pallas_call x1, Pallas kernels, project_skip(): pl.pallas_call(skip_body, in_specs=[VM, VM, VM, VM, ANY, ANY], out_specs=...  6.71 us
    pallas_call x1, Pallas kernels, project_gate(): pl.pallas_call(gate_body, in_specs=[VM, VM, VM, VM, ANY], out_specs=[VM]...  6.62 us
    pallas_call x1, Pallas kernels, inside(): pl.pallas_call(inside_body, in_specs=[ANY, VM, VM, VM], out_specs=VM, out...  5.45 us
    pallas_call x1, Pallas kernels, project_qk(): pl.pallas_call(qk_body, in_specs=[ANY] * 5, out_specs=[VM] * 5, out_shape...  5.05 us
    pallas_call x1, Pallas kernels, home(): pl.pallas_call(home_body, in_specs=[SM, ANY] + [VM] * (len(tail) + len(pi...  4.88 us
  transfers between devices with their start and end apart: 11, of which 0 were waited for; matrix products, arithmetic and copies ran while one was open for 0% of the time, Pallas kernels for 41%

commit v1 on v0

--- a/solution.py
+++ b/solution.py
@@ -67,7 +67,7 @@
     return pl.ds(pl.multiple_of(j * size, size), size)
 
 
-def qk_body(x, wq, wk, taps, streams, q_out, kt_out, x_out, taps_out, w_out, wqk, sems):
+def qk_body(x, wq, wk, taps, streams, q_out, kt_out, x_out, taps_out, w_out, choose, wqk, sems):
     feats = wq.shape[1]
     w_copies = [
         pltpu.make_async_copy(wq, wqk.at[:, 0:feats], sems.at[0]),
@@ -76,13 +76,18 @@
     x_copies = row_copies(x, x_out, sems.at[2:6], 4)
     later = columns(streams.at[0], w_out, sems.at[6:8], 0, 2)
     later.append(pltpu.make_async_copy(taps, taps_out, sems.at[8]))
-    for copy in w_copies + x_copies + later:
+    for copy in w_copies + x_copies:
         copy.start()
+    for parity in range(2):
+        choose[parity] = selection(parity)
     for copy in w_copies:
         copy.wait()
     size = x.shape[0] // 4
     for i, copy in enumerate(x_copies):
         copy.wait()
+        if i == 1:
+            for other in later:
+                other.start()
         at = slice(i * size, (i + 1) * size)
         both = dot(x_out[at], wqk[...]).astype(BF16)
         q_out[at] = both[:, :feats]
@@ -97,13 +102,14 @@
     return pl.pallas_call(
         qk_body,
         in_specs=[ANY] * 5,
-        out_specs=[VM] * 5,
+        out_specs=[VM] * 6,
         out_shape=[
             pltpu.VMEM((rows, feats), BF16),
             pltpu.VMEM((feats, rows), BF16),
             pltpu.VMEM((rows, width), BF16),
             pltpu.VMEM(conv_w.shape, F32),
             pltpu.VMEM((width, 512), BF16),
+            pltpu.VMEM((2, 128, WIDE + 128), BF16),
         ],
         scratch_shapes=[pltpu.VMEM((width, 2 * feats), BF16), pltpu.SemaphoreType.DMA((9,))],
         compiler_params=params(16),
@@ -111,68 +117,83 @@
     )(in_hbm(tokens), in_hbm(w_q), in_hbm(w_k), in_hbm(conv_w), streams)
 
 
-def convolve(halo, x, w, taps, stream, j, hold, out):
-    rows = x.shape[0]
-    at = tile(j)
-    hold[0:8] = dot(halo[...], w).astype(BF16).astype(F32)
-    for a in range(0, rows, 256):
-        hold[8 + a : 264 + a] = dot(x[a : a + 256], w).astype(BF16).astype(F32)
-    for a in range(0, rows, 256):
-        out[a : a + 256, at] = (
-            taps[0, stream, :, at] * hold[8 + a : 264 + a]
-            + taps[1, stream, :, at] * hold[7 + a : 263 + a]
-            + taps[2, stream, :, at] * hold[6 + a : 262 + a]
-        ).astype(BF16)
-
-
-def key_features(kt, dup, g):
-    size = kt.shape[1]
-    heads = pl.ds(g * PER, PER)
-    own = dup[heads, 0:F]
-    slabs = [(own * dup[heads, r : r + F]).astype(BF16) for r in range(8)]
+def project(halo, x, w, c, hold):
+    if c == 0:
+        hold[0:8] = dot(halo[...], w).astype(BF16).astype(F32)
+    at = c * CHUNK
+    hold[8 + at : 264 + at] = dot(x[at : at + CHUNK], w).astype(BF16).astype(F32)
+
+
+def filtered(taps, stream, cols, hold, c):
+    at = c * CHUNK
+    return (
+        taps[0, stream, :, cols] * hold[8 + at : 264 + at]
+        + taps[1, stream, :, cols] * hold[7 + at : 263 + at]
+        + taps[2, stream, :, cols] * hold[6 + at : 262 + at]
+    ).astype(BF16)
+
+
+def cols_of(j):
+    return slice(j * 256, (j + 1) * 256)
+
+
+def two_stages(count, chunks, first, second):
+    for j in range(count + 1):
+        for c in range(chunks):
+            if j < count:
+                first(j, c)
+            if j > 0:
+                second(j - 1, c)
+
+
+def key_features(kt, dup, g, at):
+    heads = slice(g * PER, (g + 1) * PER)
+    own = dup[heads, 0:F, at]
+    slabs = [(own * dup[heads, r : r + F, at]).astype(BF16) for r in range(8)]
     row = lax.broadcasted_iota(jnp.int32, own.shape, 1)
-    last = jnp.where(row < 8, own * dup[heads, 8 : 8 + F], 0.0)
+    last = jnp.where(row < 8, own * dup[heads, 8 : 8 + F, at], 0.0)
     slabs.append(jnp.where(row == 8, 1.0, last).astype(BF16))
-    slabs.append(kt[tile(g, 64)].reshape(PER, F, size))
-    return jnp.concatenate([s.reshape(PER * F, size) for s in slabs], axis=0)
+    slabs.append(kt[g * 64 : (g + 1) * 64, at].reshape(PER, F, CHUNK))
+    return jnp.concatenate([s.reshape(PER * F, CHUNK) for s in slabs], axis=0)
 
 
 def values_body(place, halo_in, x, w_early, streams, taps, kt, v_out, before, halo, w_next, *rest):
-    pieces, (hold, dup, flat, w_late, sems) = rest[:-5], rest[-5:]
+    pieces, (holds, dup, flat, w_late, sems) = rest[:-5], rest[-5:]
     n = len(pieces)
     rows = x.shape[0]
-    ahead = pltpu.make_async_copy(halo_in, halo, sems.at[6])
     late = columns(streams.at[0], w_late, sems.at[0:2], 2, 2)
     following = row_copies(streams.at[1], w_next, sems.at[2:6], 4)
-    for copy in [ahead] + late + following:
+    for copy in late + following:
         copy.start()
+    halo[...] = halo_in[...]
     whole = kt[...].astype(F32).reshape(H, F, rows)
     dup[:, 0:F] = whole
     dup[:, F : 2 * F] = whole
     low = lanes((SLABS, F, 128)) < 64
-    ahead.wait()
-
-    def group(w_ref, first, j, carry):
-        g = first + j
-        convolve(halo, x, w_ref[:, tile(j)], taps, 0, g, hold, v_out)
-        feats = key_features(kt, dup, g)
-        left = right = jnp.zeros((ROWS, 128), F32)
-        for c in range(rows // CHUNK):
-            at = slice(c * CHUNK, (c + 1) * CHUNK)
-            before[c, g, :, :128] = left.astype(BF16)
-            before[c, g, :, 128:] = right.astype(BF16)
-            state = dot(feats[:, at], v_out[at, tile(g)])
-            state = state.reshape(SLABS, PER, F, 256)
-            left += jnp.where(low, state[:, 0, :, :128], state[:, 1, :, :128]).reshape(ROWS, 128)
-            right += jnp.where(low, state[:, 2, :, 128:], state[:, 3, :, 128:]).reshape(ROWS, 128)
-        flat[g, :, :128] = left.astype(BF16)
-        flat[g, :, 128:] = right.astype(BF16)
-        return carry
-
-    lax.fori_loop(0, 2, functools.partial(group, w_early, 0), 0)
-    for copy in late:
-        copy.wait()
-    lax.fori_loop(0, 2, functools.partial(group, w_late, 2), 0)
+    sums = {}
+
+    def first(g, c):
+        if g >= 2 and c == 0:
+            late[g - 2].wait()
+        w = w_early[:, cols_of(g)] if g < 2 else w_late[:, cols_of(g - 2)]
+        project(halo, x, w, c, holds.at[g % 2])
+
+    def second(g, c):
+        at = slice(c * CHUNK, (c + 1) * CHUNK)
+        values = filtered(taps, 0, cols_of(g), holds.at[g % 2], c)
+        v_out[at, cols_of(g)] = values
+        left, right = sums.pop(g) if c else (jnp.zeros((ROWS, 128), F32),) * 2
+        before[c, g, :, :128] = left.astype(BF16)
+        before[c, g, :, 128:] = right.astype(BF16)
+        state = dot(key_features(kt, dup, g, at), values).reshape(SLABS, PER, F, 256)
+        left += jnp.where(low, state[:, 0, :, :128], state[:, 1, :, :128]).reshape(ROWS, 128)
+        right += jnp.where(low, state[:, 2, :, 128:], state[:, 3, :, 128:]).reshape(ROWS, 128)
+        sums[g] = left, right
+        if c == rows // CHUNK - 1:
+            flat[g, :, :128] = left.astype(BF16)
+            flat[g, :, 128:] = right.astype(BF16)
+
+    two_stages(GROUPS, rows // CHUNK, first, second)
     split = flat.reshape(n, GROUPS * ROWS // n, 256)
     for m, piece in enumerate(pieces):
         piece[...] = split[lax.rem(place[0] + m, n)]
@@ -186,7 +207,7 @@
     part = GROUPS * ROWS // n
     return pl.pallas_call(
         values_body,
-        in_specs=[SM, ANY, VM, VM, ANY, VM, VM],
+        in_specs=[SM, VM, VM, VM, ANY, VM, VM],
         out_specs=[VM] * (4 + n),
         out_shape=[
             pltpu.VMEM((rows, half), BF16),
@@ -196,27 +217,33 @@
         ]
         + [jax.ShapeDtypeStruct((part, 256), BF16) for _ in range(n)],
         scratch_shapes=[
-            pltpu.VMEM((rows + 8, 256), F32),
+            pltpu.VMEM((2, rows + 8, 256), F32),
             pltpu.VMEM((H, 2 * F, rows), F32),
             pltpu.VMEM((GROUPS, ROWS, 256), BF16),
             pltpu.VMEM((width, 512), BF16),
-            pltpu.SemaphoreType.DMA((7,)),
+            pltpu.SemaphoreType.DMA((6,)),
         ],
         compiler_params=params(20),
         name="project_values",
     )(place, halo, x, w_early, streams, taps, kt)
 
 
+def stream(number, halo, x, w, taps, out, hold):
+    chunks = x.shape[0] // CHUNK
+    for j in range(w.shape[1] // 256):
+        for c in range(chunks + 1):
+            if c < chunks:
+                project(halo, x, w[:, cols_of(j)], c, hold)
+            if c > 0:
+                at = slice((c - 1) * CHUNK, c * CHUNK)
+                out[at, cols_of(j)] = filtered(taps, number, cols_of(j), hold, c - 1)
+
+
 def gate_body(halo, x, w, taps, streams, out, w_next, hold, sems):
     copies = row_copies(streams.at[2], w_next, sems, 4)
     for copy in copies:
         copy.start()
-
-    def step(j, carry):
-        convolve(halo, x, w[:, tile(j)], taps, 1, j, hold, out)
-        return carry
-
-    lax.fori_loop(0, w.shape[1] // 256, step, 0)
+    stream(1, halo, x, w, taps, out, hold)
     for copy in copies:
         copy.wait()
 
@@ -234,19 +261,12 @@
     )(halo, x, w, taps, streams)
 
 
-def skip_body(halo, x, w, taps, w_o, gain, out, w_next, gain_out, choose, hold, sems):
+def skip_body(halo, x, w, taps, w_o, gain, out, w_next, gain_out, hold, sems):
     copies = row_copies(w_o, w_next, sems.at[0:4], 4)
     copies.append(pltpu.make_async_copy(gain, gain_out, sems.at[4]))
     for copy in copies:
         copy.start()
-    for parity in range(2):
-        choose[parity] = selection(parity)
-
-    def step(j, carry):
-        convolve(halo, x, w[:, tile(j)], taps, 2, j, hold, out)
-        return carry
-
-    lax.fori_loop(0, w.shape[1] // 256, step, 0)
+    stream(2, halo, x, w, taps, out, hold)
     for copy in copies:
         copy.wait()
 
@@ -256,12 +276,11 @@
     return pl.pallas_call(
         skip_body,
         in_specs=[VM, VM, VM, VM, ANY, ANY],
-        out_specs=[VM] * 4,
+        out_specs=[VM] * 3,
         out_shape=[
             pltpu.VMEM((rows, w.shape[1]), BF16),
             pltpu.VMEM(w_o.shape, BF16),
             pltpu.VMEM(gain.shape, F32),
-            pltpu.VMEM((2, 128, WIDE + 128), BF16),
         ],
         scratch_shapes=[pltpu.VMEM((rows + 8, 256), F32), pltpu.SemaphoreType.DMA((5,))],
         compiler_params=params(16),
@@ -322,21 +341,27 @@
 
     def chunk(c, carry):
         rows = tile(c, CHUNK)
+        scores = []
         for part in range(2):
             query = q[rows, part * 128 : (part + 1) * 128] * 0.25
             stacked = jnp.concatenate(
                 [jnp.where(head == h, query, 0.0).astype(BF16) for h in range(8)], axis=0
             )
-            score = dot(stacked, kt[part * 128 : (part + 1) * 128, rows])
-            for pair in range(4):
-                both = []
-                at = part * 512 + pair * 128
-                for h in (2 * pair, 2 * pair + 1):
-                    x = score[h * CHUNK : (h + 1) * CHUNK]
-                    poly = x * (0.5 * x + 1.0) + 1.0
-                    weight = jnp.where(causal, poly, 0.0).astype(BF16)
-                    both.append(dot(weight, v[rows, at : at + 128]))
-                out[rows, at : at + 128] = jnp.where(low, both[0], both[1])
+            scores.append(dot(stacked, kt[part * 128 : (part + 1) * 128, rows]))
+
+        def weight(h):
+            x = scores[h // 8][h % 8 * CHUNK : (h % 8 + 1) * CHUNK]
+            poly = x * (0.5 * x + 1.0) + 1.0
+            return jnp.where(causal, poly, 0.0).astype(BF16)
+
+        ready = weight(0)
+        done = []
+        for h in range(H):
+            now, ready = ready, weight(h + 1) if h + 1 < H else None
+            at = h // 2 * 128
+            done.append(dot(now, v[rows, at : at + 128]))
+            if h % 2:
+                out[rows, at : at + 128] = jnp.where(low, done[h - 1], done[h])
         return carry
 
     lax.fori_loop(0, q.shape[0] // CHUNK, chunk, 0)
@@ -366,31 +391,49 @@
     return jnp.where(src == want, scale, 0.0).astype(BF16)
 
 
-def mix(start, base, c, q, att, before, gate, skip, gain, choose, mixed):
-    rows = tile(base + c, CHUNK)
+def mix(start, base, chunks, q, att, before, gate, skip, gain, choose, mixed):
     lane = lanes((CHUNK, 128))
     one = jnp.where((lane < 64) & (lane % F == 8), 1.0, 0.0)
-    wide = lanes((SLABS, F, 256)) // 64
+    wide = lanes((1, 256)) // 64
+    masks = [jnp.where(wide == h, 1.0, 0.0).astype(BF16) for h in range(PER)]
     mean = lax.broadcasted_iota(jnp.int32, (256, 256), 0) // 64 == lanes((256, 256)) // 64
     mean = jnp.where(mean, 1.0 / 64, 0.0).astype(BF16)
-    for g in range(GROUPS):
-        query = q[rows, g // 2 * 128 : g // 2 * 128 + 128]
-        b = dot(query, choose[g % 2])
+    units = [(c, g) for c in range(chunks) for g in range(GROUPS)]
+    factors, whole, mean_sq = {}, {}, {}
+
+    def expand(u):
+        c, g = units[u]
+        query = q[tile(base + c), g // 2 * 128 : g // 2 * 128 + 128]
+        factors[u] = dot(query, choose[g % 2])
+
+    def carried(u):
+        c, g = units[u]
+        b = factors.pop(u)
         a = b[:, WIDE:]
         feats = [(a * b[:, s * 128 : (s + 1) * 128]).astype(BF16) for s in range(4)]
         b4 = b[:, 512:640]
         feats.append((jnp.where(lane < 64, a * b4, b4) + one).astype(BF16))
         state = (start[g].astype(F32) + before[base + c, g].astype(F32)).astype(BF16)
         state = state.reshape(SLABS, F, 256)
-        state = jnp.stack([jnp.where(wide == h, state, 0.0).astype(BF16) for h in range(PER)], axis=1)
-        at = slice(g * 256, (g + 1) * 256)
-        whole = att[rows, at] + dot(jnp.concatenate(feats, axis=1), state.reshape(WIDE, 256))
-        mean_sq = dot((whole * whole).astype(BF16), mean)
-        normed = (whole * lax.rsqrt(mean_sq + EPS)).astype(BF16).astype(F32)
+        state = jnp.stack([state * mask for mask in masks], axis=1).reshape(WIDE, 256)
+        whole[u] = att[tile(base + c), cols_of(g)] + dot(jnp.concatenate(feats, axis=1), state)
+
+    def squares(u):
+        mean_sq[u] = dot((whole[u] * whole[u]).astype(BF16), mean)
+
+    def gated(u):
+        c, g = units[u]
+        rows, at = tile(base + c), cols_of(g)
+        normed = (whole.pop(u) * lax.rsqrt(mean_sq.pop(u) + EPS)).astype(BF16).astype(F32)
         gates = gate[rows, at].astype(F32)
         act = 0.5 * gates * (1.0 + jnp.tanh(0.5 * gates))
         made = act * (normed * gain[:, at] + skip[rows, at].astype(F32))
-        mixed[tile(c, CHUNK), at] = made.astype(BF16)
+        mixed[c * CHUNK : (c + 1) * CHUNK, at] = made.astype(BF16)
+
+    for t in range(len(units) + 3):
+        for lag, stage in enumerate((expand, carried, squares, gated)):
+            if 0 <= t - lag < len(units):
+                stage(t - lag)
 
 
 def gather_start(place, pieces, start):
@@ -403,12 +446,8 @@
 def away_body(place, q, att, before, gate, skip, gain, choose, w_o, *rest):
     pieces, (out, start, mixed) = rest[:-3], rest[-3:]
     gather_start(place, pieces, start)
-
-    def chunk(c, carry):
-        mix(start, place[1], c, q, att, before, gate, skip, gain, choose, mixed)
-        return carry
-
-    lax.fori_loop(0, out.shape[0] // CHUNK, chunk, 0)
+    chunks = out.shape[0] // CHUNK
+    mix(start, place[1], chunks, q, att, before, gate, skip, gain, choose, mixed)
 
     def columns_of(j, carry):
         out[:, tile(j, 512)] = dot(mixed[...], w_o[:, tile(j, 512)]).astype(BF16)
@@ -420,12 +459,8 @@
 def home_body(place, after, q, att, before, gate, skip, gain, choose, *rest):
     pieces, (mixed, start) = rest[:-2], rest[-2:]
     gather_start(place, pieces, start)
-
-    def chunk(c, carry):
-        mix(start, place[2], c, q, att, before, gate, skip, gain, choose, mixed)
-        return carry
-
-    lax.fori_loop(0, mixed.shape[0] // CHUNK, chunk, 0)
+    chunks = mixed.shape[0] // CHUNK
+    mix(start, place[2], chunks, q, att, before, gate, skip, gain, choose, mixed)
 
 
 def away(place, tail, w_o, pieces, rows):
@@ -500,16 +535,16 @@
     w_out = in_hbm(w_o.reshape(half, width))
 
     halo = shift(tokens[rows - 8 :], ("chain", "ctx"), 1, n * blocks)
-    q, kt, x, taps, w_early = project_qk(tokens, w_q, w_k, conv_w, streams)
+    q, kt, x, taps, w_early, choose = project_qk(tokens, w_q, w_k, conv_w, streams)
     values, before, halo, w_gate, *mine = project_values(
-        place, in_hbm(halo), x, w_early, streams, taps, kt, n
+        place, halo, x, w_early, streams, taps, kt, n
     )
     theirs = [mine[0]] + [turn(mine[m], "ctx", m, n) for m in range(1, n)]
     gate, w_skip = project_gate(halo, x, w_gate, taps, streams)
     theirs, gate = lax.optimization_barrier((theirs, gate))
     total = add_up(theirs)
     earlier = [turn(total, "chain", d, blocks) for d in range(1, blocks)]
-    skip, weight, gains, choose = project_skip(halo, x, w_skip, taps, w_out, in_hbm(gain))
+    skip, weight, gains = project_skip(halo, x, w_skip, taps, w_out, in_hbm(gain))
     earlier, skip = lax.optimization_barrier((earlier, skip))
     starts = start_states(place, theirs, earlier)
     got = [starts[0]] + [turn(starts[m], "ctx", m, n) for m in range(1, n)]

time: 70.9 us -> 67.9 us (0.958)
  Pallas kernels: 50.4 us -> 47.1 us
    pallas_call x1, Pallas kernels: 4.88 us -> 3.23 us  [home(): pl.pallas_call(home_body, in_specs=[SM, ANY] + [VM] * (len(tail) + len(pi...]
    pallas_call x1, Pallas kernels: 7.72 us -> 6.1 us  [away(): pl.pallas_call(away_body, in_specs=[SM] + [VM] * (len(tail) + 1 + len(pie...]
  transfers between devices with their start and end apart: 11 -> 11, of which waited for: 0 -> 1; matrix products, arithmetic and copies ran while one was open for 0% -> 0% of each run, Pallas kernels for 41% -> 41%
where the time goes in v1:
time: 67.9 us; the launch traced here: 67.3 us
  Pallas kernels  47.1 us (69%)
  starting transfers between devices  18.5 us (27%)
  local copies, waits for them, and re-layouts  0.76 us (1%)
    ppermute x9, starting transfers between devices, turn(): lax.ppermute(block, axis, [(i, (i + distance) % size) for i in range(size)])  11 us
    pallas_call x1, Pallas kernels, project_values(): pl.pallas_call(values_body, in_specs=[SM, VM, VM, VM, ANY, VM, VM], out_s...  9.35 us
    pallas_call x1, Pallas kernels, project_skip(): pl.pallas_call(skip_body, in_specs=[VM, VM, VM, VM, ANY, ANY], out_specs=...  7.28 us
    pallas_call x1, Pallas kernels, project_gate(): pl.pallas_call(gate_body, in_specs=[VM, VM, VM, VM, ANY], out_specs=[VM]...  6.89 us
    pallas_call x1, Pallas kernels, away(): pl.pallas_call(away_body, in_specs=[SM] + [VM] * (len(tail) + 1 + len(pie...  6.1 us
    pallas_call x1, Pallas kernels, inside(): pl.pallas_call(inside_body, in_specs=[ANY, VM, VM, VM], out_specs=VM, out...  5.1 us
    pallas_call x1, Pallas kernels, project_qk(): pl.pallas_call(qk_body, in_specs=[ANY] * 5, out_specs=[VM] * 6, out_shape...  5.05 us
    ppermute x1, starting transfers between devices, shift(): lax.ppermute(block, axes, [(i, i + distance) for i in range(size - distan...  3.93 us
  transfers between devices with their start and end apart: 11, of which 1 were waited for; matrix products, arithmetic and copies ran while one was open for 0% of the time, Pallas kernels for 41%

profile of v1, /device:TPU:1, one launch (start us, length us, event | category | flops | bytes accessed | tf_op | source)
XLA Modules:
  0.0 67.3 jit_solution(2945336594768557038)
XLA Ops:
  0.0 0.8 %slice.3 = bf16[8,2048]{1,0:T(8,128)(2,1)S(1)} slice(bf16[1024,2048]{1,0:T(8,128)(2,1)} %x.1), slice={[1016:1024], [0:2048]} | slice | bytes 65536 | tf_op jit(solution)/shard_map/slice | solution.py:537
  0.8 3.9 %collective-permute-start = (bf16[8,2048]{1,0:T(8,128)(2,1)S(1)}, bf16[8,2048]{1,0:T(8,128)(2,1)S(1)}, u32[]{:S(2)}, u32[]{:S(2)}) collective-permute-start(bf16[8,2048]{1,0:T(8,128)(2,1)S(1)} %slice.3), channel_id=1, source_target_pairs={{0,2},{2,4},{4,6},{6,8},{8,10},{10,12},{12,14},{14,16},{16,18},{18... | collective-permute-start | bytes 98312 | tf_op jit(solution)/shard_map/ppermute | solution.py:519
  4.7 0.1 pad_add_fusion.place
  4.8 5.1 %project_qk.1 = (bf16[1024,256]{1,0:T(8,128)(2,1)S(1)}, bf16[256,1024]{1,0:T(8,128)(2,1)S(1)}, bf16[1024,2048]{1,0:T(8,128)(2,1)S(1)}, f32[3,3,1,1024]{3,2,1,0:T...) custom-call(bf16[1024,2048]{1,0:T(8,128)(2,1)} %x.1, bf16[2048,256]{1,0:T(8,128)(2,1)} %wq.1, ...), custom_call_target="tpu_custom_call" | custom-call | tf_op jit(solution)/shard_map/project_qk/pallas_call | solution.py:102
  9.9 0.0 collective-permute-done.halo_in
  9.9 9.3 %project_values.1 = (bf16[1024,1024]{1,0:T(8,128)(2,1)S(1)}, bf16[4,4,160,256]{3,2,1,0:T(8,128)(2,1)S(1)}, bf16[8,2048]{1,0:T(8,128)(2,1)S(1)}, bf16[2048,1024]{...) custom-call(s32[4]{0:T(128)S(1)} %pad_add_fusion.place, ...), custom_call_target="tpu_custom_call" | custom-call | tf_op jit(solution)/shard_map/project_values/pallas_call | solution.py:208
  19.2 1.3 %collective-permute-start.1 = (bf16[160,256]{1,0:T(8,128)(2,1)S(1)}, bf16[160,256]{1,0:T(8,128)(2,1)S(1)}, u32[]{:S(2)}, u32[]{:S(2)}) collective-permute-start(bf16[160,256]{1,0:T(8,128)(2,1)S(1)} %get-tuple-element.48), channel_id=1, source_target_pairs={{0,2},{2,4},{4,6},{6,0},{1,3},{3,5},{5,7},{7,1},{8,10},{10,12},{12... | collective-permute-start | bytes 245768 | tf_op jit(solution)/shard_map/ppermute | solution.py:523
  20.5 1.2 %collective-permute-start.2 = (bf16[160,256]{1,0:T(8,128)(2,1)S(1)}, bf16[160,256]{1,0:T(8,128)(2,1)S(1)}, u32[]{:S(2)}, u32[]{:S(2)}) collective-permute-start(bf16[160,256]{1,0:T(8,128)(2,1)S(1)} %get-tuple-element.49), channel_id=1, source_target_pairs={{0,4},{2,6},{4,0},{6,2},{1,5},{3,7},{5,1},{7,3},{8,12},{10,14},{12... | collective-permute-start | bytes 245768 | tf_op jit(solution)/shard_map/ppermute | solution.py:523
  21.7 1.2 %collective-permute-start.3 = (bf16[160,256]{1,0:T(8,128)(2,1)S(1)}, bf16[160,256]{1,0:T(8,128)(2,1)S(1)}, u32[]{:S(2)}, u32[]{:S(2)}) collective-permute-start(bf16[160,256]{1,0:T(8,128)(2,1)S(1)} %get-tuple-element.50), channel_id=1, source_target_pairs={{0,6},{2,0},{4,2},{6,4},{1,7},{3,1},{5,3},{7,5},{8,14},{10,8},{12,... | collective-permute-start | bytes 245768 | tf_op jit(solution)/shard_map/ppermute | solution.py:523
  22.9 6.9 %project_gate.1 = (bf16[1024,1024]{1,0:T(8,128)(2,1)S(1)}, bf16[2048,1024]{1,0:T(8,128)(2,1)S(1)}) custom-call(bf16[8,2048]{1,0:T(8,128)(2,1)S(1)} %get-tuple-element.51.halo, bf16[1024,2048]{1,0:T(8,128)(2,1)S(1)} %get-tuple-element.43.x, bf16[2048,1024]{1,0:T(8,128)(2,1)S(1)} %get-tuple-element.52.w, f32[3,3,1,1024]{3,2,1,0:T(1,128)S(1)} %get-tuple-element.45.taps, ...), custom_call_target="tpu_custom_call" | custom-call | tf_op jit(solution)/shard_map/project_gate/pallas_call | solution.py:253
  29.8 0.0 collective-permute-done.1.refs_1_
  29.8 0.0 collective-permute-done.2.refs_2_
  29.8 0.0 collective-permute-done.3.refs_3_
  29.9 1.4 %collective-permute-start.4 = (bf16[160,256]{1,0:T(8,128)(2,1)S(1)}, bf16[160,256]{1,0:T(8,128)(2,1)S(1)}, u32[]{:S(2)}, u32[]{:S(2)}) collective-permute-start(bf16[160,256]{1,0:T(8,128)(2,1)S(1)} %add_up.1), channel_id=1, source_target_pairs={{0,8},{8,16},{16,24},{24,0},{1,9},{9,17},{17,25},{25,1},{2,10},{10... | collective-permute-start | bytes 245768 | tf_op jit(solution)/shard_map/ppermute | solution.py:523
  31.2 2.3 %collective-permute-start.5 = (bf16[160,256]{1,0:T(8,128)(2,1)S(1)}, bf16[160,256]{1,0:T(8,128)(2,1)S(1)}, u32[]{:S(2)}, u32[]{:S(2)}) collective-permute-start(bf16[160,256]{1,0:T(8,128)(2,1)S(1)} %add_up.1), channel_id=1, source_target_pairs={{0,16},{8,24},{16,0},{24,8},{1,17},{9,25},{17,1},{25,9},{2,18},{10... | collective-permute-start | bytes 245768 | tf_op jit(solution)/shard_map/ppermute | solution.py:523
  33.5 1.1 %collective-permute-start.6 = (bf16[160,256]{1,0:T(8,128)(2,1)S(1)}, bf16[160,256]{1,0:T(8,128)(2,1)S(1)}, u32[]{:S(2)}, u32[]{:S(2)}) collective-permute-start(bf16[160,256]{1,0:T(8,128)(2,1)S(1)} %add_up.1), channel_id=1, source_target_pairs={{0,24},{8,0},{16,8},{24,16},{1,25},{9,1},{17,9},{25,17},{2,26},{10... | collective-permute-start | bytes 245768 | tf_op jit(solution)/shard_map/ppermute | solution.py:523
  34.6 7.3 %project_skip.1 = (bf16[1024,1024]{1,0:T(8,128)(2,1)S(1)}, bf16[1024,2048]{1,0:T(8,128)(2,1)S(1)}, f32[1,1024]{1,0:T(1,128)S(1)}) custom-call(bf16[8,2048]{1,0:T(8,128)(2,1)S(1)} %get-tuple-element.51.halo, bf16[1024,2048]{1,0:T(8,128)(2,1)S(1)} %get-tuple-element.43.x, bf16[2048,1024]{1,0:T(8,128)(2,1)S(1)} %get-tuple-element.58.w, ...), custom_call_target="tpu_custom_call" | custom-call | tf_op jit(solution)/shard_map/project_skip/pallas_call | solution.py:276
  41.9 0.0 collective-permute-done.4.refs_4_
  41.9 0.0 collective-permute-done.5.refs_5_
  41.9 0.0 collective-permute-done.6.refs_6_
  41.9 0.7 %start_states.1 = (bf16[160,256]{1,0:T(8,128)(2,1)S(1)}, bf16[160,256]{1,0:T(8,128)(2,1)S(1)}, bf16[160,256]{1,0:T(8,128)(2,1)S(1)}, bf16[160,256]{1,0:T(8,128)(2,1)S(1)}) custom-call(s32[4]{0:T(128)S(1)} %pad_add_fusion.place, bf16[160,256]{1,0:T(8,128)(2,1)S(1)} %get-tuple-element.54.refs_0_, bf16[160,256]{1,0:T(8,128)(2,1)S(1)} %collective-permute-done.1.refs_1_, ...), custom_call_target="tpu_custom_call" | custom-call | tf_op jit(solution)/shard_map/start_states/pallas_call | solution.py:326
  42.6 0.4 collective-permute-start.7
  43.0 0.2 collective-permute-start.8
  43.2 2.0 %collective-permute-start.9 = (bf16[160,256]{1,0:T(8,128)(2,1)S(1)}, bf16[160,256]{1,0:T(8,128)(2,1)S(1)}, u32[]{:S(2)}, u32[]{:S(2)}) collective-permute-start(bf16[160,256]{1,0:T(8,128)(2,1)S(1)} %get-tuple-element.66), channel_id=1, source_target_pairs={{0,6},{2,0},{4,2},{6,4},{1,7},{3,1},{5,3},{7,5},{8,14},{10,8},{12,... | collective-permute-start | bytes 245768 | tf_op jit(solution)/shard_map/ppermute | solution.py:523
  45.3 5.1 %inside.1.att = f32[1024,1024]{1,0:T(8,128)S(1)} custom-call(bf16[160,256]{1,0:T(8,128)(2,1)S(1)} %get-tuple-element.75.after.rest_0_, bf16[1024,256]{1,0:T(8,128)(2,1)S(1)} %get-tuple-element.42.q, bf16[256,1024]{1,0:T(8,128)(2,1)S(1)} %get-tuple-element.46.kt, bf16[1024,1024]{1,0:T(8,128)(2,1)S(1)} %get-tuple-element.67.v), custom_call_target="tpu_custom_call" | custom-call | tf_op jit(solution)/shard_map/inside/pallas_call | solution.py:371
  50.4 0.0 collective-permute-done.7.rest_1_
  50.4 0.0 collective-permute-done.8.rest_2_
  50.4 0.0 collective-permute-done.9.rest_3_
  50.4 6.1 %away.1.after = bf16[512,2048]{1,0:T(8,128)(2,1)S(1)} custom-call(s32[4]{0:T(128)S(1)} %pad_add_fusion.place, bf16[1024,256]{1,0:T(8,128)(2,1)S(1)} %get-tuple-element.42.q, f32[1024,1024]{1,0:T(8,128)S(1)} %inside.1.att, bf16[4,4,160,256]{3,2,1,0:T(8,128)(2,1)S(1)} %get-tuple-element.69.before, bf16[1024,1024]{1,0:T(8,128)(2,1)S(1)} %get-tuple-element.70.gate, ...), custom_call_target="tpu_custom_call" | custom-call | tf_op jit(solution)/shard_map/away/pallas_call | solution.py:468
  56.5 3.5 %collective-permute-start.10 = (bf16[512,2048]{1,0:T(8,128)(2,1)S(1)}, bf16[512,2048]{1,0:T(8,128)(2,1)S(1)}, u32[]{:S(2)}, u32[]{:S(2)}) collective-permute-start(bf16[512,2048]{1,0:T(8,128)(2,1)S(1)} %away.1.after), channel_id=1, source_target_pairs={{0,1},{1,0},{2,3},{3,2},{4,5},{5,4},{6,7},{7,6},{8,9},{9,8},{10,11... | collective-permute-start | bytes 6291464 | tf_op jit(solution)/shard_map/ppermute | solution.py:555
  60.1 3.2 %home.1.mixed = bf16[512,1024]{1,0:T(8,128)(2,1)S(1)} custom-call(s32[4]{0:T(128)S(1)} %pad_add_fusion.place, bf16[512,2048]{1,0:T(8,128)(2,1)S(1)} %away.1.after, bf16[1024,256]{1,0:T(8,128)(2,1)S(1)} %get-tuple-element.42.q, f32[1024,1024]{1,0:T(8,128)S(1)} %inside.1.att, bf16[4,4,160,256]{3,2,1,0:T(8,128)(2,1)S(1)} %get-tuple-element.69.before, ...), custom_call_target="tpu_custom_call" | custom-call | tf_op jit(solution)/shard_map/home/pallas_call | solution.py:480
  63.3 0.5 collective-permute-done.10.other
  63.9 3.3 %join.1 = bf16[512,2048]{1,0:T(8,128)(2,1)} custom-call(bf16[512,1024]{1,0:T(8,128)(2,1)S(1)} %home.1.mixed, bf16[1024,2048]{1,0:T(8,128)(2,1)S(1)} %get-tuple-element.74.w_o, bf16[512,2048]{1,0:T(8,128)(2,1)S(1)} %collective-permute-done.10.other), custom_call_target="tpu_custom_call" | custom-call | tf_op jit(solution)/shard_map/join/pallas_call | solution.py:504
  (1 shorter events, 0.0 us)
Async XLA Ops:
  0.8 9.1 %collective-permute-start = (bf16[8,2048]{1,0:T(8,128)(2,1)S(1)}, bf16[8,2048]{1,0:T(8,128)(2,1)S(1)}, u32[]{:S(2)}, u32[]{:S(2)}) collective-permute-start(bf16[8,2048]{1,0:T(8,128)(2,1)S(1)} %slice.3), channel_id=1, source_target_pairs={{0,2},{2,4},{4,6},{6,8},{8,10},{10,12},{12,14},{14,16},{16,18},{18... | collective-permute-start | bytes 98312 | tf_op jit(solution)/shard_map/ppermute | solution.py:519
  19.2 10.6 %collective-permute-start.1 = (bf16[160,256]{1,0:T(8,128)(2,1)S(1)}, bf16[160,256]{1,0:T(8,128)(2,1)S(1)}, u32[]{:S(2)}, u32[]{:S(2)}) collective-permute-start(bf16[160,256]{1,0:T(8,128)(2,1)S(1)} %get-tuple-element.48), channel_id=1, source_target_pairs={{0,2},{2,4},{4,6},{6,0},{1,3},{3,5},{5,7},{7,1},{8,10},{10,12},{12... | collective-permute-start | bytes 245768 | tf_op jit(solution)/shard_map/ppermute | solution.py:523
  20.5 9.3 %collective-permute-start.2 = (bf16[160,256]{1,0:T(8,128)(2,1)S(1)}, bf16[160,256]{1,0:T(8,128)(2,1)S(1)}, u32[]{:S(2)}, u32[]{:S(2)}) collective-permute-start(bf16[160,256]{1,0:T(8,128)(2,1)S(1)} %get-tuple-element.49), channel_id=1, source_target_pairs={{0,4},{2,6},{4,0},{6,2},{1,5},{3,7},{5,1},{7,3},{8,12},{10,14},{12... | collective-permute-start | bytes 245768 | tf_op jit(solution)/shard_map/ppermute | solution.py:523
  21.7 8.1 %collective-permute-start.3 = (bf16[160,256]{1,0:T(8,128)(2,1)S(1)}, bf16[160,256]{1,0:T(8,128)(2,1)S(1)}, u32[]{:S(2)}, u32[]{:S(2)}) collective-permute-start(bf16[160,256]{1,0:T(8,128)(2,1)S(1)} %get-tuple-element.50), channel_id=1, source_target_pairs={{0,6},{2,0},{4,2},{6,4},{1,7},{3,1},{5,3},{7,5},{8,14},{10,8},{12,... | collective-permute-start | bytes 245768 | tf_op jit(solution)/shard_map/ppermute | solution.py:523
  29.9 12.0 %collective-permute-start.4 = (bf16[160,256]{1,0:T(8,128)(2,1)S(1)}, bf16[160,256]{1,0:T(8,128)(2,1)S(1)}, u32[]{:S(2)}, u32[]{:S(2)}) collective-permute-start(bf16[160,256]{1,0:T(8,128)(2,1)S(1)} %add_up.1), channel_id=1, source_target_pairs={{0,8},{8,16},{16,24},{24,0},{1,9},{9,17},{17,25},{25,1},{2,10},{10... | collective-permute-start | bytes 245768 | tf_op jit(solution)/shard_map/ppermute | solution.py:523
  31.2 10.7 %collective-permute-start.5 = (bf16[160,256]{1,0:T(8,128)(2,1)S(1)}, bf16[160,256]{1,0:T(8,128)(2,1)S(1)}, u32[]{:S(2)}, u32[]{:S(2)}) collective-permute-start(bf16[160,256]{1,0:T(8,128)(2,1)S(1)} %add_up.1), channel_id=1, source_target_pairs={{0,16},{8,24},{16,0},{24,8},{1,17},{9,25},{17,1},{25,9},{2,18},{10... | collective-permute-start | bytes 245768 | tf_op jit(solution)/shard_map/ppermute | solution.py:523
  33.5 8.4 %collective-permute-start.6 = (bf16[160,256]{1,0:T(8,128)(2,1)S(1)}, bf16[160,256]{1,0:T(8,128)(2,1)S(1)}, u32[]{:S(2)}, u32[]{:S(2)}) collective-permute-start(bf16[160,256]{1,0:T(8,128)(2,1)S(1)} %add_up.1), channel_id=1, source_target_pairs={{0,24},{8,0},{16,8},{24,16},{1,25},{9,1},{17,9},{25,17},{2,26},{10... | collective-permute-start | bytes 245768 | tf_op jit(solution)/shard_map/ppermute | solution.py:523
  42.6 7.8 %collective-permute-start.7 = (bf16[160,256]{1,0:T(8,128)(2,1)S(1)}, bf16[160,256]{1,0:T(8,128)(2,1)S(1)}, u32[]{:S(2)}, u32[]{:S(2)}) collective-permute-start(bf16[160,256]{1,0:T(8,128)(2,1)S(1)} %get-tuple-element.64), channel_id=1, source_target_pairs={{0,2},{2,4},{4,6},{6,0},{1,3},{3,5},{5,7},{7,1},{8,10},{10,12},{12... | collective-permute-start | bytes 245768 | tf_op jit(solution)/shard_map/ppermute | solution.py:523
  43.0 7.4 %collective-permute-start.8 = (bf16[160,256]{1,0:T(8,128)(2,1)S(1)}, bf16[160,256]{1,0:T(8,128)(2,1)S(1)}, u32[]{:S(2)}, u32[]{:S(2)}) collective-permute-start(bf16[160,256]{1,0:T(8,128)(2,1)S(1)} %get-tuple-element.65), channel_id=1, source_target_pairs={{0,4},{2,6},{4,0},{6,2},{1,5},{3,7},{5,1},{7,3},{8,12},{10,14},{12... | collective-permute-start | bytes 245768 | tf_op jit(solution)/shard_map/ppermute | solution.py:523
  43.2 7.2 %collective-permute-start.9 = (bf16[160,256]{1,0:T(8,128)(2,1)S(1)}, bf16[160,256]{1,0:T(8,128)(2,1)S(1)}, u32[]{:S(2)}, u32[]{:S(2)}) collective-permute-start(bf16[160,256]{1,0:T(8,128)(2,1)S(1)} %get-tuple-element.66), channel_id=1, source_target_pairs={{0,6},{2,0},{4,2},{6,4},{1,7},{3,1},{5,3},{7,5},{8,14},{10,8},{12,... | collective-permute-start | bytes 245768 | tf_op jit(solution)/shard_map/ppermute | solution.py:523
  56.5 7.3 %collective-permute-start.10 = (bf16[512,2048]{1,0:T(8,128)(2,1)S(1)}, bf16[512,2048]{1,0:T(8,128)(2,1)S(1)}, u32[]{:S(2)}, u32[]{:S(2)}) collective-permute-start(bf16[512,2048]{1,0:T(8,128)(2,1)S(1)} %away.1.after), channel_id=1, source_target_pairs={{0,1},{1,0},{2,3},{3,2},{4,5},{5,4},{6,7},{7,6},{8,9},{9,8},{10,11... | collective-permute-start | bytes 6291464 | tf_op jit(solution)/shard_map/ppermute | solution.py:555

commit v2 on v1

--- a/solution.py
+++ b/solution.py
@@ -34,15 +34,9 @@
     return pltpu.with_memory_space_constraint(x, pltpu.HBM)
 
 
-def columns(src, dst, sems, first, count, at=0):
-    return [
-        pltpu.make_async_copy(
-            src.at[:, (first + j) * 256 : (first + j + 1) * 256],
-            dst.at[:, (at + j) * 256 : (at + j + 1) * 256],
-            sems.at[j],
-        )
-        for j in range(count)
-    ]
+def half_copy(src, dst, sem, part):
+    size = dst.shape[1]
+    return pltpu.make_async_copy(src.at[:, part * size : (part + 1) * size], dst, sem)
 
 
 def row_copies(src, dst, sems, count):
@@ -74,14 +68,15 @@
         pltpu.make_async_copy(wk, wqk.at[:, feats : 2 * feats], sems.at[1]),
     ]
     x_copies = row_copies(x, x_out, sems.at[2:6], 4)
-    later = columns(streams.at[0], w_out, sems.at[6:8], 0, 2)
-    later.append(pltpu.make_async_copy(taps, taps_out, sems.at[8]))
+    later = [half_copy(streams.at[0], w_out, sems.at[6], 0)]
+    later.append(pltpu.make_async_copy(taps, taps_out, sems.at[7]))
     for copy in w_copies + x_copies:
         copy.start()
     for parity in range(2):
         choose[parity] = selection(parity)
     for copy in w_copies:
         copy.wait()
+    w = wqk[...]
     size = x.shape[0] // 4
     for i, copy in enumerate(x_copies):
         copy.wait()
@@ -89,7 +84,7 @@
             for other in later:
                 other.start()
         at = slice(i * size, (i + 1) * size)
-        both = dot(x_out[at], wqk[...]).astype(BF16)
+        both = dot(x_out[at], w).astype(BF16)
         q_out[at] = both[:, :feats]
         kt_out[:, at] = both[:, feats:].astype(F32).T.astype(BF16)
     for copy in later:
@@ -111,7 +106,10 @@
             pltpu.VMEM((width, 512), BF16),
             pltpu.VMEM((2, 128, WIDE + 128), BF16),
         ],
-        scratch_shapes=[pltpu.VMEM((width, 2 * feats), BF16), pltpu.SemaphoreType.DMA((9,))],
+        scratch_shapes=[
+            pltpu.VMEM((width, 2 * feats), BF16),
+            pltpu.SemaphoreType.DMA((8,)),
+        ],
         compiler_params=params(16),
         name="project_qk",
     )(in_hbm(tokens), in_hbm(w_q), in_hbm(w_k), in_hbm(conv_w), streams)
@@ -137,13 +135,14 @@
     return slice(j * 256, (j + 1) * 256)
 
 
-def two_stages(count, chunks, first, second):
-    for j in range(count + 1):
-        for c in range(chunks):
-            if j < count:
-                first(j, c)
-            if j > 0:
-                second(j - 1, c)
+def stream_tile(number, j, halo, x, w, taps, out, hold):
+    chunks = x.shape[0] // CHUNK
+    for c in range(chunks + 1):
+        if c < chunks:
+            project(halo, x, w, c, hold)
+        if c > 0:
+            at = slice((c - 1) * CHUNK, c * CHUNK)
+            out[at, cols_of(j)] = filtered(taps, number, cols_of(j), hold, c - 1)
 
 
 def key_features(kt, dup, g, at):
@@ -161,39 +160,37 @@
     pieces, (holds, dup, flat, w_late, sems) = rest[:-5], rest[-5:]
     n = len(pieces)
     rows = x.shape[0]
-    late = columns(streams.at[0], w_late, sems.at[0:2], 2, 2)
-    following = row_copies(streams.at[1], w_next, sems.at[2:6], 4)
-    for copy in late + following:
+    late = half_copy(streams.at[0], w_late, sems.at[0], 1)
+    following = row_copies(streams.at[1], w_next, sems.at[1:5], 4)
+    for copy in [late] + following:
         copy.start()
     halo[...] = halo_in[...]
     whole = kt[...].astype(F32).reshape(H, F, rows)
     dup[:, 0:F] = whole
     dup[:, F : 2 * F] = whole
     low = lanes((SLABS, F, 128)) < 64
-    sums = {}
-
-    def first(g, c):
-        if g >= 2 and c == 0:
-            late[g - 2].wait()
+    chunks = [slice(at, at + CHUNK) for at in range(0, rows, CHUNK)]
+
+    def states(g):
+        left = right = jnp.zeros((ROWS, 128), F32)
+        for c, at in enumerate(chunks):
+            before[c, g, :, :128] = left.astype(BF16)
+            before[c, g, :, 128:] = right.astype(BF16)
+            state = dot(key_features(kt, dup, g, at), v_out[at, cols_of(g)])
+            state = state.reshape(SLABS, PER, F, 256)
+            left += jnp.where(low, state[:, 0, :, :128], state[:, 1, :, :128]).reshape(ROWS, 128)
+            right += jnp.where(low, state[:, 2, :, 128:], state[:, 3, :, 128:]).reshape(ROWS, 128)
+        flat[g, :, :128] = left.astype(BF16)
+        flat[g, :, 128:] = right.astype(BF16)
+
+    for g in range(GROUPS):
+        if g == 2:
+            late.wait()
         w = w_early[:, cols_of(g)] if g < 2 else w_late[:, cols_of(g - 2)]
-        project(halo, x, w, c, holds.at[g % 2])
-
-    def second(g, c):
-        at = slice(c * CHUNK, (c + 1) * CHUNK)
-        values = filtered(taps, 0, cols_of(g), holds.at[g % 2], c)
-        v_out[at, cols_of(g)] = values
-        left, right = sums.pop(g) if c else (jnp.zeros((ROWS, 128), F32),) * 2
-        before[c, g, :, :128] = left.astype(BF16)
-        before[c, g, :, 128:] = right.astype(BF16)
-        state = dot(key_features(kt, dup, g, at), values).reshape(SLABS, PER, F, 256)
-        left += jnp.where(low, state[:, 0, :, :128], state[:, 1, :, :128]).reshape(ROWS, 128)
-        right += jnp.where(low, state[:, 2, :, 128:], state[:, 3, :, 128:]).reshape(ROWS, 128)
-        sums[g] = left, right
-        if c == rows // CHUNK - 1:
-            flat[g, :, :128] = left.astype(BF16)
-            flat[g, :, 128:] = right.astype(BF16)
-
-    two_stages(GROUPS, rows // CHUNK, first, second)
+        stream_tile(0, g, halo, x, w, taps, v_out, holds.at[g % 2])
+        if g > 0:
+            states(g - 1)
+    states(GROUPS - 1)
     split = flat.reshape(n, GROUPS * ROWS // n, 256)
     for m, piece in enumerate(pieces):
         piece[...] = split[lax.rem(place[0] + m, n)]
@@ -221,7 +218,7 @@
             pltpu.VMEM((H, 2 * F, rows), F32),
             pltpu.VMEM((GROUPS, ROWS, 256), BF16),
             pltpu.VMEM((width, 512), BF16),
-            pltpu.SemaphoreType.DMA((6,)),
+            pltpu.SemaphoreType.DMA((5,)),
         ],
         compiler_params=params(20),
         name="project_values",
@@ -229,14 +226,8 @@
 
 
 def stream(number, halo, x, w, taps, out, hold):
-    chunks = x.shape[0] // CHUNK
     for j in range(w.shape[1] // 256):
-        for c in range(chunks + 1):
-            if c < chunks:
-                project(halo, x, w[:, cols_of(j)], c, hold)
-            if c > 0:
-                at = slice((c - 1) * CHUNK, c * CHUNK)
-                out[at, cols_of(j)] = filtered(taps, number, cols_of(j), hold, c - 1)
+        stream_tile(number, j, halo, x, w[:, cols_of(j)], taps, out, hold)
 
 
 def gate_body(halo, x, w, taps, streams, out, w_next, hold, sems):
@@ -391,7 +382,7 @@
     return jnp.where(src == want, scale, 0.0).astype(BF16)
 
 
-def mix(start, base, chunks, q, att, before, gate, skip, gain, choose, mixed):
+def mix(start, base, chunks, q, att, before, gate, skip, gain, choose, w_o, mixed, out):
     lane = lanes((CHUNK, 128))
     one = jnp.where((lane < 64) & (lane % F == 8), 1.0, 0.0)
     wide = lanes((1, 256)) // 64
@@ -430,8 +421,14 @@
         made = act * (normed * gain[:, at] + skip[rows, at].astype(F32))
         mixed[c * CHUNK : (c + 1) * CHUNK, at] = made.astype(BF16)
 
-    for t in range(len(units) + 3):
-        for lag, stage in enumerate((expand, carried, squares, gated)):
+    def product(u):
+        c, j = units[u]
+        rows, at = slice(c * CHUNK, (c + 1) * CHUNK), slice(j * 512, (j + 1) * 512)
+        out[rows, at] = dot(mixed[rows], w_o[:, at]).astype(BF16)
+
+    stages = ((expand, 0), (carried, 1), (squares, 2), (gated, 3), (product, 3 + GROUPS))
+    for t in range(len(units) + 3 + GROUPS):
+        for stage, lag in stages:
             if 0 <= t - lag < len(units):
                 stage(t - lag)
 
@@ -443,76 +440,48 @@
         split[lax.rem(place[0] + n - m, n)] = piece[...]
 
 
-def away_body(place, q, att, before, gate, skip, gain, choose, w_o, *rest):
+def finish_body(which, place, after, q, att, before, gate, skip, gain, choose, w_o, *rest):
     pieces, (out, start, mixed) = rest[:-3], rest[-3:]
     gather_start(place, pieces, start)
     chunks = out.shape[0] // CHUNK
-    mix(start, place[1], chunks, q, att, before, gate, skip, gain, choose, mixed)
-
-    def columns_of(j, carry):
-        out[:, tile(j, 512)] = dot(mixed[...], w_o[:, tile(j, 512)]).astype(BF16)
-        return carry
-
-    lax.fori_loop(0, out.shape[1] // 512, columns_of, 0)
-
-
-def home_body(place, after, q, att, before, gate, skip, gain, choose, *rest):
-    pieces, (mixed, start) = rest[:-2], rest[-2:]
-    gather_start(place, pieces, start)
-    chunks = mixed.shape[0] // CHUNK
-    mix(start, place[2], chunks, q, att, before, gate, skip, gain, choose, mixed)
-
-
-def away(place, tail, w_o, pieces, rows):
+    mix(start, place[which], chunks, q, att, before, gate, skip, gain, choose, w_o, mixed, out)
+
+
+def finish(which, place, after, tail, w_o, pieces, rows):
     half, width = w_o.shape
     return pl.pallas_call(
-        away_body,
-        in_specs=[SM] + [VM] * (len(tail) + 1 + len(pieces)),
+        functools.partial(finish_body, which),
+        in_specs=[SM, ANY] + [VM] * (len(tail) + 1 + len(pieces)),
         out_specs=VM,
-        out_shape=jax.ShapeDtypeStruct((rows, width), BF16),
+        out_shape=pltpu.VMEM((rows, width), BF16),
         scratch_shapes=[pltpu.VMEM((GROUPS, ROWS, 256), BF16), pltpu.VMEM((rows, half), BF16)],
         compiler_params=params(16),
-        name="away",
-    )(place, *tail, w_o, *pieces)
-
-
-def home(place, after, tail, pieces, rows, half):
-    return pl.pallas_call(
-        home_body,
-        in_specs=[SM, ANY] + [VM] * (len(tail) + len(pieces)),
-        out_specs=VM,
-        out_shape=pltpu.VMEM((rows, half), BF16),
-        scratch_shapes=[pltpu.VMEM((GROUPS, ROWS, 256), BF16)],
-        compiler_params=params(16),
-        name="home",
-    )(place, after, *tail, *pieces)
-
-
-def join_body(mixed, w_o, other, out, hold, sems):
+        name="away" if which == 1 else "home",
+    )(place, after, *tail, w_o, *pieces)
+
+
+def join_body(own, other, out, hold, sems):
     copies = []
-    for j in range(out.shape[1] // 512):
-        at = slice(j * 512, (j + 1) * 512)
-        own = dot(mixed[...], w_o[:, at]).astype(BF16).astype(F32)
-        hold[:, at] = (own + other[:, at].astype(F32)).astype(BF16)
-        copies.append(pltpu.make_async_copy(hold.at[:, at], out.at[:, at], sems.at[j]))
+    size = out.shape[0] // 8
+    for i in range(8):
+        at = slice(i * size, (i + 1) * size)
+        hold[at] = (own[at].astype(F32) + other[at].astype(F32)).astype(BF16)
+        copies.append(pltpu.make_async_copy(hold.at[at], out.at[at], sems.at[i]))
         copies[-1].start()
     for copy in copies:
         copy.wait()
 
 
-def join(mixed, w_o, other):
+def join(own, other):
     return pl.pallas_call(
         join_body,
-        in_specs=[VM, VM, VM],
+        in_specs=[VM, VM],
         out_specs=pl.BlockSpec(memory_space=pltpu.HBM),
         out_shape=jax.ShapeDtypeStruct(other.shape, BF16),
-        scratch_shapes=[
-            pltpu.VMEM(other.shape, BF16),
-            pltpu.SemaphoreType.DMA((other.shape[1] // 512,)),
-        ],
-        compiler_params=params(16),
+        scratch_shapes=[pltpu.VMEM(other.shape, BF16), pltpu.SemaphoreType.DMA((8,))],
+        compiler_params=params(8),
         name="join",
-    )(mixed, w_o, other)
+    )(own, other)
 
 
 def shift(block, axes, distance, size):
@@ -551,10 +520,10 @@
     att = inside(starts[0], q, kt, values)
     got, att = lax.optimization_barrier((got, att))
     tail = (q, att, before, gate, skip, gains, choose)
-    sent = away(place, tail, weight, got, rows // 2)
+    sent = finish(1, place, att, tail, weight, got, rows // 2)
     swapped = lax.ppermute(sent, "tp", [(0, 1), (1, 0)])
-    mixed = home(place, sent, tail, got, rows // 2, half)
-    return join(mixed, weight, swapped)
+    kept = finish(2, place, sent, tail, weight, got, rows // 2)
+    return join(kept, swapped)
 
 
 def solution(mesh):

time: 67.9 us -> 62.9 us (0.926)
  Pallas kernels: 47.1 us -> 43 us
    pallas_call x1, Pallas kernels: 7.28 us -> 5.7 us  [project_skip(): pl.pallas_call(skip_body, in_specs=[VM, VM, VM, VM, ANY, ANY], out_specs=...]
    pallas_call x1, Pallas kernels: 6.89 us -> 5.68 us  [project_gate(): pl.pallas_call(gate_body, in_specs=[VM, VM, VM, VM, ANY], out_specs=[VM]...]
    pallas_call x1, Pallas kernels: 9.35 us -> 8.57 us  [project_values(): pl.pallas_call(values_body, in_specs=[SM, VM, VM, VM, ANY, VM, VM], out_s...]
  transfers between devices with their start and end apart: 11 -> 11, of which waited for: 1 -> 0; matrix products, arithmetic and copies ran while one was open for 0% -> 0% of each run, Pallas kernels for 41% -> 43%
where the time goes in v2:
time: 62.9 us; the launch traced here: 62.7 us
  Pallas kernels  43 us (68%)
  starting transfers between devices  18.5 us (29%)
  local copies, waits for them, and re-layouts  0.76 us (1%)
    ppermute x9, starting transfers between devices, turn(): lax.ppermute(block, axis, [(i, (i + distance) % size) for i in range(size)])  11 us
    pallas_call x2, Pallas kernels, finish(): pl.pallas_call(functools.partial(finish_body, which), in_specs=[SM, ANY]...  10.6 us
    pallas_call x1, Pallas kernels, project_values(): pl.pallas_call(values_body, in_specs=[SM, VM, VM, VM, ANY, VM, VM], out_s...  8.57 us
    pallas_call x1, Pallas kernels, project_skip(): pl.pallas_call(skip_body, in_specs=[VM, VM, VM, VM, ANY, ANY], out_specs=...  5.7 us
    pallas_call x1, Pallas kernels, project_gate(): pl.pallas_call(gate_body, in_specs=[VM, VM, VM, VM, ANY], out_specs=[VM]...  5.68 us
    pallas_call x1, Pallas kernels, inside(): pl.pallas_call(inside_body, in_specs=[ANY, VM, VM, VM], out_specs=VM, out...  5.1 us
    pallas_call x1, Pallas kernels, project_qk(): pl.pallas_call(qk_body, in_specs=[ANY] * 5, out_specs=[VM] * 6, out_shape...  5.1 us
    ppermute x1, starting transfers between devices, shift(): lax.ppermute(block, axes, [(i, i + distance) for i in range(size - distan...  3.93 us
  transfers between devices with their start and end apart: 11, of which 0 were waited for; matrix products, arithmetic and copies ran while one was open for 0% of the time, Pallas kernels for 43%

profile of v2, /device:TPU:1, one launch (start us, length us, event | category | flops | bytes accessed | tf_op | source)
XLA Modules:
  0.0 62.7 jit_solution(15114679799708025189)
XLA Ops:
  0.0 0.8 %slice.3 = bf16[8,2048]{1,0:T(8,128)(2,1)S(1)} slice(bf16[1024,2048]{1,0:T(8,128)(2,1)} %x.1), slice={[1016:1024], [0:2048]} | slice | bytes 65536 | tf_op jit(solution)/shard_map/slice | solution.py:506
  0.8 3.9 %collective-permute-start = (bf16[8,2048]{1,0:T(8,128)(2,1)S(1)}, bf16[8,2048]{1,0:T(8,128)(2,1)S(1)}, u32[]{:S(2)}, u32[]{:S(2)}) collective-permute-start(bf16[8,2048]{1,0:T(8,128)(2,1)S(1)} %slice.3), channel_id=1, source_target_pairs={{0,2},{2,4},{4,6},{6,8},{8,10},{10,12},{12,14},{14,16},{16,18},{18... | collective-permute-start | bytes 98312 | tf_op jit(solution)/shard_map/ppermute | solution.py:488
  4.7 0.1 pad_add_fusion.place
  4.8 5.1 %project_qk.1 = (bf16[1024,256]{1,0:T(8,128)(2,1)S(1)}, bf16[256,1024]{1,0:T(8,128)(2,1)S(1)}, bf16[1024,2048]{1,0:T(8,128)(2,1)S(1)}, f32[3,3,1,1024]{3,2,1,0:T...) custom-call(bf16[1024,2048]{1,0:T(8,128)(2,1)} %x.1, bf16[2048,256]{1,0:T(8,128)(2,1)} %wq.1, ...), custom_call_target="tpu_custom_call" | custom-call | tf_op jit(solution)/shard_map/project_qk/pallas_call | solution.py:97
  9.9 0.0 collective-permute-done.halo_in
  9.9 8.6 %project_values.1 = (bf16[1024,1024]{1,0:T(8,128)(2,1)S(1)}, bf16[4,4,160,256]{3,2,1,0:T(8,128)(2,1)S(1)}, bf16[8,2048]{1,0:T(8,128)(2,1)S(1)}, bf16[2048,1024]{...) custom-call(s32[4]{0:T(128)S(1)} %pad_add_fusion.place, ...), custom_call_target="tpu_custom_call" | custom-call | tf_op jit(solution)/shard_map/project_values/pallas_call | solution.py:205
  18.5 1.3 %collective-permute-start.1 = (bf16[160,256]{1,0:T(8,128)(2,1)S(1)}, bf16[160,256]{1,0:T(8,128)(2,1)S(1)}, u32[]{:S(2)}, u32[]{:S(2)}) collective-permute-start(bf16[160,256]{1,0:T(8,128)(2,1)S(1)} %get-tuple-element.47), channel_id=1, source_target_pairs={{0,2},{2,4},{4,6},{6,0},{1,3},{3,5},{5,7},{7,1},{8,10},{10,12},{12... | collective-permute-start | bytes 245768 | tf_op jit(solution)/shard_map/ppermute | solution.py:492
  19.7 1.2 %collective-permute-start.2 = (bf16[160,256]{1,0:T(8,128)(2,1)S(1)}, bf16[160,256]{1,0:T(8,128)(2,1)S(1)}, u32[]{:S(2)}, u32[]{:S(2)}) collective-permute-start(bf16[160,256]{1,0:T(8,128)(2,1)S(1)} %get-tuple-element.48), channel_id=1, source_target_pairs={{0,4},{2,6},{4,0},{6,2},{1,5},{3,7},{5,1},{7,3},{8,12},{10,14},{12... | collective-permute-start | bytes 245768 | tf_op jit(solution)/shard_map/ppermute | solution.py:492
  21.0 1.1 %collective-permute-start.3 = (bf16[160,256]{1,0:T(8,128)(2,1)S(1)}, bf16[160,256]{1,0:T(8,128)(2,1)S(1)}, u32[]{:S(2)}, u32[]{:S(2)}) collective-permute-start(bf16[160,256]{1,0:T(8,128)(2,1)S(1)} %get-tuple-element.49), channel_id=1, source_target_pairs={{0,6},{2,0},{4,2},{6,4},{1,7},{3,1},{5,3},{7,5},{8,14},{10,8},{12,... | collective-permute-start | bytes 245768 | tf_op jit(solution)/shard_map/ppermute | solution.py:492
  22.1 5.7 %project_gate.1 = (bf16[1024,1024]{1,0:T(8,128)(2,1)S(1)}, bf16[2048,1024]{1,0:T(8,128)(2,1)S(1)}) custom-call(bf16[8,2048]{1,0:T(8,128)(2,1)S(1)} %get-tuple-element.50.halo, bf16[1024,2048]{1,0:T(8,128)(2,1)S(1)} %get-tuple-element.42.x, bf16[2048,1024]{1,0:T(8,128)(2,1)S(1)} %get-tuple-element.51.w, f32[3,3,1,1024]{3,2,1,0:T(1,128)S(1)} %get-tuple-element.44.taps, ...), custom_call_target="tpu_custom_call" | custom-call | tf_op jit(solution)/shard_map/project_gate/pallas_call | solution.py:244
  27.8 0.0 collective-permute-done.1.refs_1_
  27.8 0.0 collective-permute-done.2.refs_2_
  27.8 0.0 collective-permute-done.3.refs_3_
  27.9 1.4 %collective-permute-start.4 = (bf16[160,256]{1,0:T(8,128)(2,1)S(1)}, bf16[160,256]{1,0:T(8,128)(2,1)S(1)}, u32[]{:S(2)}, u32[]{:S(2)}) collective-permute-start(bf16[160,256]{1,0:T(8,128)(2,1)S(1)} %add_up.1), channel_id=1, source_target_pairs={{0,8},{8,16},{16,24},{24,0},{1,9},{9,17},{17,25},{25,1},{2,10},{10... | collective-permute-start | bytes 245768 | tf_op jit(solution)/shard_map/ppermute | solution.py:492
  29.3 2.3 %collective-permute-start.5 = (bf16[160,256]{1,0:T(8,128)(2,1)S(1)}, bf16[160,256]{1,0:T(8,128)(2,1)S(1)}, u32[]{:S(2)}, u32[]{:S(2)}) collective-permute-start(bf16[160,256]{1,0:T(8,128)(2,1)S(1)} %add_up.1), channel_id=1, source_target_pairs={{0,16},{8,24},{16,0},{24,8},{1,17},{9,25},{17,1},{25,9},{2,18},{10... | collective-permute-start | bytes 245768 | tf_op jit(solution)/shard_map/ppermute | solution.py:492
  31.6 1.1 %collective-permute-start.6 = (bf16[160,256]{1,0:T(8,128)(2,1)S(1)}, bf16[160,256]{1,0:T(8,128)(2,1)S(1)}, u32[]{:S(2)}, u32[]{:S(2)}) collective-permute-start(bf16[160,256]{1,0:T(8,128)(2,1)S(1)} %add_up.1), channel_id=1, source_target_pairs={{0,24},{8,0},{16,8},{24,16},{1,25},{9,1},{17,9},{25,17},{2,26},{10... | collective-permute-start | bytes 245768 | tf_op jit(solution)/shard_map/ppermute | solution.py:492
  32.6 5.7 %project_skip.1 = (bf16[1024,1024]{1,0:T(8,128)(2,1)S(1)}, bf16[1024,2048]{1,0:T(8,128)(2,1)S(1)}, f32[1,1024]{1,0:T(1,128)S(1)}) custom-call(bf16[8,2048]{1,0:T(8,128)(2,1)S(1)} %get-tuple-element.50.halo, bf16[1024,2048]{1,0:T(8,128)(2,1)S(1)} %get-tuple-element.42.x, bf16[2048,1024]{1,0:T(8,128)(2,1)S(1)} %get-tuple-element.57.w, ...), custom_call_target="tpu_custom_call" | custom-call | tf_op jit(solution)/shard_map/project_skip/pallas_call | solution.py:267
  38.4 0.0 collective-permute-done.4.refs_4_
  38.4 0.0 collective-permute-done.5.refs_5_
  38.4 0.0 collective-permute-done.6.refs_6_
  38.4 0.7 %start_states.1 = (bf16[160,256]{1,0:T(8,128)(2,1)S(1)}, bf16[160,256]{1,0:T(8,128)(2,1)S(1)}, bf16[160,256]{1,0:T(8,128)(2,1)S(1)}, bf16[160,256]{1,0:T(8,128)(2,1)S(1)}) custom-call(s32[4]{0:T(128)S(1)} %pad_add_fusion.place, bf16[160,256]{1,0:T(8,128)(2,1)S(1)} %get-tuple-element.53.refs_0_, bf16[160,256]{1,0:T(8,128)(2,1)S(1)} %collective-permute-done.1.refs_1_, ...), custom_call_target="tpu_custom_call" | custom-call | tf_op jit(solution)/shard_map/start_states/pallas_call | solution.py:317
  39.1 0.4 collective-permute-start.7
  39.5 0.2 collective-permute-start.8
  39.7 2.1 %collective-permute-start.9 = (bf16[160,256]{1,0:T(8,128)(2,1)S(1)}, bf16[160,256]{1,0:T(8,128)(2,1)S(1)}, u32[]{:S(2)}, u32[]{:S(2)}) collective-permute-start(bf16[160,256]{1,0:T(8,128)(2,1)S(1)} %get-tuple-element.65), channel_id=1, source_target_pairs={{0,6},{2,0},{4,2},{6,4},{1,7},{3,1},{5,3},{7,5},{8,14},{10,8},{12,... | collective-permute-start | bytes 245768 | tf_op jit(solution)/shard_map/ppermute | solution.py:492
  41.8 5.1 %inside.1.after.att = f32[1024,1024]{1,0:T(8,128)S(1)} custom-call(bf16[160,256]{1,0:T(8,128)(2,1)S(1)} %get-tuple-element.75.after.rest_0_, bf16[1024,256]{1,0:T(8,128)(2,1)S(1)} %get-tuple-element.66.q, bf16[256,1024]{1,0:T(8,128)(2,1)S(1)} %get-tuple-element.45.kt, bf16[1024,1024]{1,0:T(8,128)(2,1)S(1)} %get-tuple-element.67.v), custom_call_target="tpu_custom_call" | custom-call | tf_op jit(solution)/shard_map/inside/pallas_call | solution.py:362
  46.9 0.0 collective-permute-done.7.rest_1_
  46.9 0.0 collective-permute-done.8.rest_2_
  46.9 0.0 collective-permute-done.9.rest_3_
  46.9 5.3 %away.1.after = bf16[512,2048]{1,0:T(8,128)(2,1)S(1)} custom-call(s32[4]{0:T(128)S(1)} %pad_add_fusion.place, f32[1024,1024]{1,0:T(8,128)S(1)} %inside.1.after.att, bf16[1024,256]{1,0:T(8,128)(2,1)S(1)} %get-tuple-element.66.q, f32[1024,1024]{1,0:T(8,128)S(1)} %inside.1.after.att, bf16[4,4,160,256]{3,2,1,0:T(8,128)(2,1)S(1)} %get-tuple-element.69.before, ...), custom_call_target="tpu_custom_call" | custom-call | tf_op jit(solution)/shard_map/away/pallas_call | solution.py:452
  52.2 3.5 %collective-permute-start.10 = (bf16[512,2048]{1,0:T(8,128)(2,1)S(1)}, bf16[512,2048]{1,0:T(8,128)(2,1)S(1)}, u32[]{:S(2)}, u32[]{:S(2)}) collective-permute-start(bf16[512,2048]{1,0:T(8,128)(2,1)S(1)} %away.1.after), channel_id=1, source_target_pairs={{0,1},{1,0},{2,3},{3,2},{4,5},{5,4},{6,7},{7,6},{8,9},{9,8},{10,11... | collective-permute-start | bytes 6291464 | tf_op jit(solution)/shard_map/ppermute | solution.py:524
  55.7 5.3 %home.1.own = bf16[512,2048]{1,0:T(8,128)(2,1)S(1)} custom-call(s32[4]{0:T(128)S(1)} %pad_add_fusion.place, bf16[512,2048]{1,0:T(8,128)(2,1)S(1)} %away.1.after, bf16[1024,256]{1,0:T(8,128)(2,1)S(1)} %get-tuple-element.66.q, f32[1024,1024]{1,0:T(8,128)S(1)} %inside.1.after.att, bf16[4,4,160,256]{3,2,1,0:T(8,128)(2,1)S(1)} %get-tuple-element.69.before, ...), custom_call_target="tpu_custom_call" | custom-call | tf_op jit(solution)/shard_map/home/pallas_call | solution.py:452
  61.0 0.0 collective-permute-done.10.other
  61.0 1.4 %join.1 = bf16[512,2048]{1,0:T(8,128)(2,1)} custom-call(bf16[512,2048]{1,0:T(8,128)(2,1)S(1)} %home.1.own, bf16[512,2048]{1,0:T(8,128)(2,1)S(1)} %collective-permute-done.10.other), custom_call_target="tpu_custom_call" | custom-call | tf_op jit(solution)/shard_map/join/pallas_call | solution.py:476
  (1 shorter events, 0.0 us)
Async XLA Ops:
  0.8 9.1 %collective-permute-start = (bf16[8,2048]{1,0:T(8,128)(2,1)S(1)}, bf16[8,2048]{1,0:T(8,128)(2,1)S(1)}, u32[]{:S(2)}, u32[]{:S(2)}) collective-permute-start(bf16[8,2048]{1,0:T(8,128)(2,1)S(1)} %slice.3), channel_id=1, source_target_pairs={{0,2},{2,4},{4,6},{6,8},{8,10},{10,12},{12,14},{14,16},{16,18},{18... | collective-permute-start | bytes 98312 | tf_op jit(solution)/shard_map/ppermute | solution.py:488
  18.5 9.3 %collective-permute-start.1 = (bf16[160,256]{1,0:T(8,128)(2,1)S(1)}, bf16[160,256]{1,0:T(8,128)(2,1)S(1)}, u32[]{:S(2)}, u32[]{:S(2)}) collective-permute-start(bf16[160,256]{1,0:T(8,128)(2,1)S(1)} %get-tuple-element.47), channel_id=1, source_target_pairs={{0,2},{2,4},{4,6},{6,0},{1,3},{3,5},{5,7},{7,1},{8,10},{10,12},{12... | collective-permute-start | bytes 245768 | tf_op jit(solution)/shard_map/ppermute | solution.py:492
  19.7 8.1 %collective-permute-start.2 = (bf16[160,256]{1,0:T(8,128)(2,1)S(1)}, bf16[160,256]{1,0:T(8,128)(2,1)S(1)}, u32[]{:S(2)}, u32[]{:S(2)}) collective-permute-start(bf16[160,256]{1,0:T(8,128)(2,1)S(1)} %get-tuple-element.48), channel_id=1, source_target_pairs={{0,4},{2,6},{4,0},{6,2},{1,5},{3,7},{5,1},{7,3},{8,12},{10,14},{12... | collective-permute-start | bytes 245768 | tf_op jit(solution)/shard_map/ppermute | solution.py:492
  21.0 6.9 %collective-permute-start.3 = (bf16[160,256]{1,0:T(8,128)(2,1)S(1)}, bf16[160,256]{1,0:T(8,128)(2,1)S(1)}, u32[]{:S(2)}, u32[]{:S(2)}) collective-permute-start(bf16[160,256]{1,0:T(8,128)(2,1)S(1)} %get-tuple-element.49), channel_id=1, source_target_pairs={{0,6},{2,0},{4,2},{6,4},{1,7},{3,1},{5,3},{7,5},{8,14},{10,8},{12,... | collective-permute-start | bytes 245768 | tf_op jit(solution)/shard_map/ppermute | solution.py:492
  27.9 10.5 %collective-permute-start.4 = (bf16[160,256]{1,0:T(8,128)(2,1)S(1)}, bf16[160,256]{1,0:T(8,128)(2,1)S(1)}, u32[]{:S(2)}, u32[]{:S(2)}) collective-permute-start(bf16[160,256]{1,0:T(8,128)(2,1)S(1)} %add_up.1), channel_id=1, source_target_pairs={{0,8},{8,16},{16,24},{24,0},{1,9},{9,17},{17,25},{25,1},{2,10},{10... | collective-permute-start | bytes 245768 | tf_op jit(solution)/shard_map/ppermute | solution.py:492
  29.3 9.1 %collective-permute-start.5 = (bf16[160,256]{1,0:T(8,128)(2,1)S(1)}, bf16[160,256]{1,0:T(8,128)(2,1)S(1)}, u32[]{:S(2)}, u32[]{:S(2)}) collective-permute-start(bf16[160,256]{1,0:T(8,128)(2,1)S(1)} %add_up.1), channel_id=1, source_target_pairs={{0,16},{8,24},{16,0},{24,8},{1,17},{9,25},{17,1},{25,9},{2,18},{10... | collective-permute-start | bytes 245768 | tf_op jit(solution)/shard_map/ppermute | solution.py:492
  31.6 6.8 %collective-permute-start.6 = (bf16[160,256]{1,0:T(8,128)(2,1)S(1)}, bf16[160,256]{1,0:T(8,128)(2,1)S(1)}, u32[]{:S(2)}, u32[]{:S(2)}) collective-permute-start(bf16[160,256]{1,0:T(8,128)(2,1)S(1)} %add_up.1), channel_id=1, source_target_pairs={{0,24},{8,0},{16,8},{24,16},{1,25},{9,1},{17,9},{25,17},{2,26},{10... | collective-permute-start | bytes 245768 | tf_op jit(solution)/shard_map/ppermute | solution.py:492
  39.1 7.8 %collective-permute-start.7 = (bf16[160,256]{1,0:T(8,128)(2,1)S(1)}, bf16[160,256]{1,0:T(8,128)(2,1)S(1)}, u32[]{:S(2)}, u32[]{:S(2)}) collective-permute-start(bf16[160,256]{1,0:T(8,128)(2,1)S(1)} %get-tuple-element.63), channel_id=1, source_target_pairs={{0,2},{2,4},{4,6},{6,0},{1,3},{3,5},{5,7},{7,1},{8,10},{10,12},{12... | collective-permute-start | bytes 245768 | tf_op jit(solution)/shard_map/ppermute | solution.py:492
  39.5 7.4 %collective-permute-start.8 = (bf16[160,256]{1,0:T(8,128)(2,1)S(1)}, bf16[160,256]{1,0:T(8,128)(2,1)S(1)}, u32[]{:S(2)}, u32[]{:S(2)}) collective-permute-start(bf16[160,256]{1,0:T(8,128)(2,1)S(1)} %get-tuple-element.64), channel_id=1, source_target_pairs={{0,4},{2,6},{4,0},{6,2},{1,5},{3,7},{5,1},{7,3},{8,12},{10,14},{12... | collective-permute-start | bytes 245768 | tf_op jit(solution)/shard_map/ppermute | solution.py:492
  39.7 7.2 %collective-permute-start.9 = (bf16[160,256]{1,0:T(8,128)(2,1)S(1)}, bf16[160,256]{1,0:T(8,128)(2,1)S(1)}, u32[]{:S(2)}, u32[]{:S(2)}) collective-permute-start(bf16[160,256]{1,0:T(8,128)(2,1)S(1)} %get-tuple-element.65), channel_id=1, source_target_pairs={{0,6},{2,0},{4,2},{6,4},{1,7},{3,1},{5,3},{7,5},{8,14},{10,8},{12,... | collective-permute-start | bytes 245768 | tf_op jit(solution)/shard_map/ppermute | solution.py:492
  52.2 8.8 %collective-permute-start.10 = (bf16[512,2048]{1,0:T(8,128)(2,1)S(1)}, bf16[512,2048]{1,0:T(8,128)(2,1)S(1)}, u32[]{:S(2)}, u32[]{:S(2)}) collective-permute-start(bf16[512,2048]{1,0:T(8,128)(2,1)S(1)} %away.1.after), channel_id=1, source_target_pairs={{0,1},{1,0},{2,3},{3,2},{4,5},{5,4},{6,7},{7,6},{8,9},{9,8},{10,11... | collective-permute-start | bytes 6291464 | tf_op jit(solution)/shard_map/ppermute | solution.py:524

commit v3 on v2

--- a/solution.py
+++ b/solution.py
@@ -23,7 +23,6 @@
 
 VM = pl.BlockSpec(memory_space=pltpu.VMEM)
 ANY = pl.BlockSpec(memory_space=pl.ANY)
-SM = pl.BlockSpec(memory_space=pltpu.SMEM)
 
 
 def params(mib):
@@ -156,7 +155,7 @@
     return jnp.concatenate([s.reshape(PER * F, CHUNK) for s in slabs], axis=0)
 
 
-def values_body(place, halo_in, x, w_early, streams, taps, kt, v_out, before, halo, w_next, *rest):
+def values_body(halo_in, x, w_early, streams, taps, kt, v_out, before, halo, w_next, *rest):
     pieces, (holds, dup, flat, w_late, sems) = rest[:-5], rest[-5:]
     n = len(pieces)
     rows = x.shape[0]
@@ -193,18 +192,18 @@
     states(GROUPS - 1)
     split = flat.reshape(n, GROUPS * ROWS // n, 256)
     for m, piece in enumerate(pieces):
-        piece[...] = split[lax.rem(place[0] + m, n)]
+        piece[...] = split[lax.rem(lax.axis_index("ctx") + m, n)]
     for copy in following:
         copy.wait()
 
 
-def project_values(place, halo, x, w_early, streams, taps, kt, n):
+def project_values(halo, x, w_early, streams, taps, kt, n):
     rows, width = x.shape
     half = streams.shape[2]
     part = GROUPS * ROWS // n
     return pl.pallas_call(
         values_body,
-        in_specs=[SM, VM, VM, VM, ANY, VM, VM],
+        in_specs=[VM, VM, VM, ANY, VM, VM],
         out_specs=[VM] * (4 + n),
         out_shape=[
             pltpu.VMEM((rows, half), BF16),
@@ -222,7 +221,7 @@
         ],
         compiler_params=params(20),
         name="project_values",
-    )(place, halo, x, w_early, streams, taps, kt)
+    )(halo, x, w_early, streams, taps, kt)
 
 
 def stream(number, halo, x, w, taps, out, hold):
@@ -297,62 +296,79 @@
     )(*parts)
 
 
-def starts_body(n, place, *refs):
-    parts, earlier, outs, hold = refs[:n], refs[n : -n - 1], refs[-n - 1 : -1], refs[-1]
-    for k, part in enumerate(parts):
-        hold[lax.rem(place[0] + n - k, n)] = part[...].astype(F32)
-    found = jnp.zeros(parts[0].shape, F32)
+def starts_body(n, *refs):
+    parts, earlier, outs = refs[:n], refs[n:-n], refs[-n:]
+    me, block_index = lax.axis_index("ctx"), lax.axis_index("chain")
+    base = jnp.zeros(parts[0].shape, F32)
     for d, block in enumerate(earlier):
-        found += jnp.where(place[3] > d, block[...].astype(F32), 0.0)
-    for p in range(n):
-        own = hold[p]
-        hold[p] = found
-        found += own
+        base += jnp.where(block_index > d, block[...].astype(F32), 0.0)
+    known = [part[...].astype(F32) for part in parts]
     for m, out in enumerate(outs):
-        out[...] = hold[lax.rem(place[0] + m, n)].astype(BF16)
-
-
-def start_states(place, parts, earlier):
+        peer = lax.rem(me + m, n)
+        found = base
+        for k, part in enumerate(known):
+            found += jnp.where(lax.rem(me + n - k, n) < peer, part, 0.0)
+        out[...] = found.astype(BF16)
+
+
+def start_states(parts, earlier):
     n, shape = len(parts), parts[0].shape
     return pl.pallas_call(
         functools.partial(starts_body, n),
-        in_specs=[SM] + [VM] * (n + len(earlier)),
+        in_specs=[VM] * (n + len(earlier)),
         out_specs=[VM] * n,
         out_shape=[jax.ShapeDtypeStruct(shape, BF16) for _ in range(n)],
-        scratch_shapes=[pltpu.VMEM((n,) + shape, F32)],
         compiler_params=params(8),
         name="start_states",
-    )(place, *parts, *earlier)
+    )(*parts, *earlier)
 
 
 def inside_body(after, q, kt, v, out):
-    low = lanes((CHUNK, 128)) < 64
-    head = lanes((CHUNK, 128)) // F
-    causal = lax.broadcasted_iota(jnp.int32, (CHUNK, CHUNK), 0) >= lanes((CHUNK, CHUNK))
+    half = CHUNK // 2
+    lane = lanes((1, 128))
+    low = lanes((half, 128)) < 64
+    sides = [jnp.where((lane < 64) == side, 1.0, 0.0).astype(BF16) for side in (True, False)]
+    heads = [jnp.where(lane // F == h, 1.0, 0.0).astype(BF16) for h in range(8)]
+    row = lax.broadcasted_iota(jnp.int32, (128, half), 0) // F
+    keep = [jnp.where(row == h, 1.0, 0.0).astype(BF16) for h in range(8)]
+    first_row = lax.broadcasted_iota(jnp.int32, (half, CHUNK), 0)
+    seen_first = first_row >= lanes((half, CHUNK)) % half
+    seen_last = first_row + half >= lanes((half, CHUNK))
+
+    def poly(x, seen):
+        return jnp.where(seen, x * (0.5 * x + 1.0) + 1.0, 0.0).astype(BF16)
 
     def chunk(c, carry):
+        top, bottom = pl.ds(pl.multiple_of(c * CHUNK, half), half), pl.ds(
+            pl.multiple_of(c * CHUNK + half, half), half
+        )
         rows = tile(c, CHUNK)
-        scores = []
+        first, last = [], []
         for part in range(2):
-            query = q[rows, part * 128 : (part + 1) * 128] * 0.25
-            stacked = jnp.concatenate(
-                [jnp.where(head == h, query, 0.0).astype(BF16) for h in range(8)], axis=0
+            keys = kt[part * 128 : (part + 1) * 128, rows]
+            scaled = q[rows, part * 128 : (part + 1) * 128] * jnp.asarray(0.25, BF16)
+            last.append(dot(jnp.concatenate([scaled[half:] * h for h in heads], axis=0), keys))
+            for pair in range(4):
+                two = [keys[:, :half] * keep[h] for h in (2 * pair, 2 * pair + 1)]
+                first.append(dot(scaled[:half], jnp.concatenate(two, axis=1)))
+
+        def weights(p):
+            at = p % 4 * 2 * half
+            tail = last[p // 4]
+            return (
+                poly(first[p], seen_first),
+                poly(tail[at : at + half], seen_last),
+                poly(tail[at + half : at + 2 * half], seen_last),
             )
-            scores.append(dot(stacked, kt[part * 128 : (part + 1) * 128, rows]))
-
-        def weight(h):
-            x = scores[h // 8][h % 8 * CHUNK : (h % 8 + 1) * CHUNK]
-            poly = x * (0.5 * x + 1.0) + 1.0
-            return jnp.where(causal, poly, 0.0).astype(BF16)
-
-        ready = weight(0)
-        done = []
-        for h in range(H):
-            now, ready = ready, weight(h + 1) if h + 1 < H else None
-            at = h // 2 * 128
-            done.append(dot(now, v[rows, at : at + 128]))
-            if h % 2:
-                out[rows, at : at + 128] = jnp.where(low, done[h - 1], done[h])
+
+        ready = weights(0)
+        for p in range(H // 2):
+            now, ready = ready, weights(p + 1) if p + 1 < H // 2 else None
+            at = slice(p * 128, (p + 1) * 128)
+            early = v[top, at]
+            out[top, at] = dot(now[0], jnp.concatenate([early * side for side in sides], axis=0))
+            whole = v[rows, at]
+            out[bottom, at] = jnp.where(low, dot(now[1], whole), dot(now[2], whole))
         return carry
 
     lax.fori_loop(0, q.shape[0] // CHUNK, chunk, 0)
@@ -433,31 +449,33 @@
                 stage(t - lag)
 
 
-def gather_start(place, pieces, start):
+def gather_start(pieces, start):
     n = len(pieces)
     split = start.reshape(n, GROUPS * ROWS // n, 256)
     for m, piece in enumerate(pieces):
-        split[lax.rem(place[0] + n - m, n)] = piece[...]
-
-
-def finish_body(which, place, after, q, att, before, gate, skip, gain, choose, w_o, *rest):
+        split[lax.rem(lax.axis_index("ctx") + n - m, n)] = piece[...]
+
+
+def finish_body(away, after, q, att, before, gate, skip, gain, choose, w_o, *rest):
     pieces, (out, start, mixed) = rest[:-3], rest[-3:]
-    gather_start(place, pieces, start)
+    gather_start(pieces, start)
     chunks = out.shape[0] // CHUNK
-    mix(start, place[which], chunks, q, att, before, gate, skip, gain, choose, w_o, mixed, out)
-
-
-def finish(which, place, after, tail, w_o, pieces, rows):
+    core = lax.axis_index("tp")
+    base = chunks * (1 - core if away else core)
+    mix(start, base, chunks, q, att, before, gate, skip, gain, choose, w_o, mixed, out)
+
+
+def finish(away, after, tail, w_o, pieces, rows):
     half, width = w_o.shape
     return pl.pallas_call(
-        functools.partial(finish_body, which),
-        in_specs=[SM, ANY] + [VM] * (len(tail) + 1 + len(pieces)),
+        functools.partial(finish_body, away),
+        in_specs=[ANY] + [VM] * (len(tail) + 1 + len(pieces)),
         out_specs=VM,
         out_shape=pltpu.VMEM((rows, width), BF16),
         scratch_shapes=[pltpu.VMEM((GROUPS, ROWS, 256), BF16), pltpu.VMEM((rows, half), BF16)],
         compiler_params=params(16),
-        name="away" if which == 1 else "home",
-    )(place, after, *tail, w_o, *pieces)
+        name="away" if away else "home",
+    )(after, *tail, w_o, *pieces)
 
 
 def join_body(own, other, out, hold, sems):
@@ -496,17 +514,13 @@
     rows, width = tokens.shape
     half = w_in.shape[3]
     n, blocks = lax.axis_size("ctx"), lax.axis_size("chain")
-    me, core = lax.axis_index("ctx"), lax.axis_index("tp")
-    per_half = rows // CHUNK // 2
-    block = lax.axis_index("chain")
-    place = jnp.stack([me, (1 - core) * per_half, core * per_half, block]).astype(jnp.int32)
     streams = in_hbm(w_in.transpose(1, 2, 0, 3).reshape(3, width, half))
     w_out = in_hbm(w_o.reshape(half, width))
 
     halo = shift(tokens[rows - 8 :], ("chain", "ctx"), 1, n * blocks)
     q, kt, x, taps, w_early, choose = project_qk(tokens, w_q, w_k, conv_w, streams)
     values, before, halo, w_gate, *mine = project_values(
-        place, halo, x, w_early, streams, taps, kt, n
+        halo, x, w_early, streams, taps, kt, n
     )
     theirs = [mine[0]] + [turn(mine[m], "ctx", m, n) for m in range(1, n)]
     gate, w_skip = project_gate(halo, x, w_gate, taps, streams)
@@ -515,14 +529,14 @@
     earlier = [turn(total, "chain", d, blocks) for d in range(1, blocks)]
     skip, weight, gains = project_skip(halo, x, w_skip, taps, w_out, in_hbm(gain))
     earlier, skip = lax.optimization_barrier((earlier, skip))
-    starts = start_states(place, theirs, earlier)
+    starts = start_states(theirs, earlier)
     got = [starts[0]] + [turn(starts[m], "ctx", m, n) for m in range(1, n)]
     att = inside(starts[0], q, kt, values)
     got, att = lax.optimization_barrier((got, att))
     tail = (q, att, before, gate, skip, gains, choose)
-    sent = finish(1, place, att, tail, weight, got, rows // 2)
+    sent = finish(True, att, tail, weight, got, rows // 2)
     swapped = lax.ppermute(sent, "tp", [(0, 1), (1, 0)])
-    kept = finish(2, place, sent, tail, weight, got, rows // 2)
+    kept = finish(False, sent, tail, weight, got, rows // 2)
     return join(kept, swapped)
 
 

time: 62.9 us -> 59.9 us (0.952)
  Pallas kernels: 43 us -> 40.1 us
    pallas_call x4, Pallas kernels: 19.9 us -> 17.6 us  [the longest x2 9.35 us: finish(): pl.pallas_call(functools.partial(finish_body, away), in_specs=[ANY] + [VM...]
where the time goes in v3:
time: 59.9 us; the launch traced here: 59.7 us
  Pallas kernels  40.1 us (67%)
  starting transfers between devices  18.5 us (31%)
  local copies, waits for them, and re-layouts  0.76 us (1%)
    ppermute x9, starting transfers between devices, turn(): lax.ppermute(block, axis, [(i, (i + distance) % size) for i in range(size)])  11 us
    pallas_call x2, Pallas kernels, finish(): pl.pallas_call(functools.partial(finish_body, away), in_specs=[ANY] + [VM...  9.35 us
    pallas_call x1, Pallas kernels, project_values(): pl.pallas_call(values_body, in_specs=[VM, VM, VM, ANY, VM, VM], out_specs...  8.01 us
    pallas_call x1, Pallas kernels, project_skip(): pl.pallas_call(skip_body, in_specs=[VM, VM, VM, VM, ANY, ANY], out_specs=...  5.67 us
    pallas_call x1, Pallas kernels, project_gate(): pl.pallas_call(gate_body, in_specs=[VM, VM, VM, VM, ANY], out_specs=[VM]...  5.67 us
    pallas_call x1, Pallas kernels, project_qk(): pl.pallas_call(qk_body, in_specs=[ANY] * 5, out_specs=[VM] * 6, out_shape...  5.09 us
    pallas_call x1, Pallas kernels, inside(): pl.pallas_call(inside_body, in_specs=[ANY, VM, VM, VM], out_specs=VM, out...  4.6 us
    ppermute x1, starting transfers between devices, shift(): lax.ppermute(block, axes, [(i, i + distance) for i in range(size - distan...  3.93 us
  transfers between devices with their start and end apart: 11, of which 0 were waited for; matrix products, arithmetic and copies ran while one was open for 0% of the time, Pallas kernels for 43%

profile of v3, /device:TPU:1, one launch (start us, length us, event | category | flops | bytes accessed | tf_op | source)
XLA Modules:
  0.0 59.7 jit_solution(7270371623695244889)
XLA Ops:
  0.0 0.8 %slice.3 = bf16[8,2048]{1,0:T(8,128)(2,1)S(1)} slice(bf16[1024,2048]{1,0:T(8,128)(2,1)} %x.1), slice={[1016:1024], [0:2048]} | slice | bytes 65536 | tf_op jit(solution)/shard_map/slice | solution.py:520
  0.8 3.9 %collective-permute-start = (bf16[8,2048]{1,0:T(8,128)(2,1)S(1)}, bf16[8,2048]{1,0:T(8,128)(2,1)S(1)}, u32[]{:S(2)}, u32[]{:S(2)}) collective-permute-start(bf16[8,2048]{1,0:T(8,128)(2,1)S(1)} %slice.3), channel_id=1, source_target_pairs={{0,2},{2,4},{4,6},{6,8},{8,10},{10,12},{12,14},{14,16},{16,18},{18... | collective-permute-start | bytes 98312 | tf_op jit(solution)/shard_map/ppermute | solution.py:506
  4.7 5.1 %project_qk.1 = (bf16[1024,256]{1,0:T(8,128)(2,1)S(1)}, bf16[256,1024]{1,0:T(8,128)(2,1)S(1)}, bf16[1024,2048]{1,0:T(8,128)(2,1)S(1)}, f32[3,3,1,1024]{3,2,1,0:T...) custom-call(bf16[1024,2048]{1,0:T(8,128)(2,1)} %x.1, bf16[2048,256]{1,0:T(8,128)(2,1)} %wq.1, ...), custom_call_target="tpu_custom_call" | custom-call | tf_op jit(solution)/shard_map/project_qk/pallas_call | solution.py:96
  9.8 0.0 collective-permute-done.halo_in
  9.8 8.0 %project_values.1 = (bf16[1024,1024]{1,0:T(8,128)(2,1)S(1)}, bf16[4,4,160,256]{3,2,1,0:T(8,128)(2,1)S(1)}, bf16[8,2048]{1,0:T(8,128)(2,1)S(1)}, bf16[2048,1024]{...) custom-call(bf16[8,2048]{1,0:T(8,128)(2,1)S(1)} %collective-permute-, ...), custom_call_target="tpu_custom_call" | custom-call | tf_op jit(solution)/shard_map/project_values/pallas_call | solution.py:204
  17.8 1.3 %collective-permute-start.1 = (bf16[160,256]{1,0:T(8,128)(2,1)S(1)}, bf16[160,256]{1,0:T(8,128)(2,1)S(1)}, u32[]{:S(2)}, u32[]{:S(2)}) collective-permute-start(bf16[160,256]{1,0:T(8,128)(2,1)S(1)} %get-tuple-element.47), channel_id=1, source_target_pairs={{0,2},{2,4},{4,6},{6,0},{1,3},{3,5},{5,7},{7,1},{8,10},{10,12},{12... | collective-permute-start | bytes 245768 | tf_op jit(solution)/shard_map/ppermute | solution.py:510
  19.1 1.2 %collective-permute-start.2 = (bf16[160,256]{1,0:T(8,128)(2,1)S(1)}, bf16[160,256]{1,0:T(8,128)(2,1)S(1)}, u32[]{:S(2)}, u32[]{:S(2)}) collective-permute-start(bf16[160,256]{1,0:T(8,128)(2,1)S(1)} %get-tuple-element.48), channel_id=1, source_target_pairs={{0,4},{2,6},{4,0},{6,2},{1,5},{3,7},{5,1},{7,3},{8,12},{10,14},{12... | collective-permute-start | bytes 245768 | tf_op jit(solution)/shard_map/ppermute | solution.py:510
  20.3 1.1 %collective-permute-start.3 = (bf16[160,256]{1,0:T(8,128)(2,1)S(1)}, bf16[160,256]{1,0:T(8,128)(2,1)S(1)}, u32[]{:S(2)}, u32[]{:S(2)}) collective-permute-start(bf16[160,256]{1,0:T(8,128)(2,1)S(1)} %get-tuple-element.49), channel_id=1, source_target_pairs={{0,6},{2,0},{4,2},{6,4},{1,7},{3,1},{5,3},{7,5},{8,14},{10,8},{12,... | collective-permute-start | bytes 245768 | tf_op jit(solution)/shard_map/ppermute | solution.py:510
  21.5 5.7 %project_gate.1 = (bf16[1024,1024]{1,0:T(8,128)(2,1)S(1)}, bf16[2048,1024]{1,0:T(8,128)(2,1)S(1)}) custom-call(bf16[8,2048]{1,0:T(8,128)(2,1)S(1)} %get-tuple-element.50.halo, bf16[1024,2048]{1,0:T(8,128)(2,1)S(1)} %get-tuple-element.42.x, bf16[2048,1024]{1,0:T(8,128)(2,1)S(1)} %get-tuple-element.51.w, f32[3,3,1,1024]{3,2,1,0:T(1,128)S(1)} %get-tuple-element.44.taps, ...), custom_call_target="tpu_custom_call" | custom-call | tf_op jit(solution)/shard_map/project_gate/pallas_call | solution.py:243
  27.2 0.0 collective-permute-done.1.refs_1_
  27.2 0.0 collective-permute-done.2.refs_2_
  27.2 0.0 collective-permute-done.3.refs_3_
  27.2 1.4 %collective-permute-start.4 = (bf16[160,256]{1,0:T(8,128)(2,1)S(1)}, bf16[160,256]{1,0:T(8,128)(2,1)S(1)}, u32[]{:S(2)}, u32[]{:S(2)}) collective-permute-start(bf16[160,256]{1,0:T(8,128)(2,1)S(1)} %add_up.1), channel_id=1, source_target_pairs={{0,8},{8,16},{16,24},{24,0},{1,9},{9,17},{17,25},{25,1},{2,10},{10... | collective-permute-start | bytes 245768 | tf_op jit(solution)/shard_map/ppermute | solution.py:510
  28.6 2.3 %collective-permute-start.5 = (bf16[160,256]{1,0:T(8,128)(2,1)S(1)}, bf16[160,256]{1,0:T(8,128)(2,1)S(1)}, u32[]{:S(2)}, u32[]{:S(2)}) collective-permute-start(bf16[160,256]{1,0:T(8,128)(2,1)S(1)} %add_up.1), channel_id=1, source_target_pairs={{0,16},{8,24},{16,0},{24,8},{1,17},{9,25},{17,1},{25,9},{2,18},{10... | collective-permute-start | bytes 245768 | tf_op jit(solution)/shard_map/ppermute | solution.py:510
  30.9 1.1 %collective-permute-start.6 = (bf16[160,256]{1,0:T(8,128)(2,1)S(1)}, bf16[160,256]{1,0:T(8,128)(2,1)S(1)}, u32[]{:S(2)}, u32[]{:S(2)}) collective-permute-start(bf16[160,256]{1,0:T(8,128)(2,1)S(1)} %add_up.1), channel_id=1, source_target_pairs={{0,24},{8,0},{16,8},{24,16},{1,25},{9,1},{17,9},{25,17},{2,26},{10... | collective-permute-start | bytes 245768 | tf_op jit(solution)/shard_map/ppermute | solution.py:510
  32.0 5.7 %project_skip.1 = (bf16[1024,1024]{1,0:T(8,128)(2,1)S(1)}, bf16[1024,2048]{1,0:T(8,128)(2,1)S(1)}, f32[1,1024]{1,0:T(1,128)S(1)}) custom-call(bf16[8,2048]{1,0:T(8,128)(2,1)S(1)} %get-tuple-element.50.halo, bf16[1024,2048]{1,0:T(8,128)(2,1)S(1)} %get-tuple-element.42.x, bf16[2048,1024]{1,0:T(8,128)(2,1)S(1)} %get-tuple-element.57.w, ...), custom_call_target="tpu_custom_call" | custom-call | tf_op jit(solution)/shard_map/project_skip/pallas_call | solution.py:266
  37.6 0.0 collective-permute-done.4.refs_4_
  37.7 0.0 collective-permute-done.5.refs_5_
  37.7 0.0 collective-permute-done.6.refs_6_
  37.7 0.2 start_states.1
  37.9 0.4 collective-permute-start.7
  38.3 0.2 collective-permute-start.8
  38.5 2.0 %collective-permute-start.9 = (bf16[160,256]{1,0:T(8,128)(2,1)S(1)}, bf16[160,256]{1,0:T(8,128)(2,1)S(1)}, u32[]{:S(2)}, u32[]{:S(2)}) collective-permute-start(bf16[160,256]{1,0:T(8,128)(2,1)S(1)} %get-tuple-element.65), channel_id=1, source_target_pairs={{0,6},{2,0},{4,2},{6,4},{1,7},{3,1},{5,3},{7,5},{8,14},{10,8},{12,... | collective-permute-start | bytes 245768 | tf_op jit(solution)/shard_map/ppermute | solution.py:510
  40.6 4.6 %inside.1.after.att = f32[1024,1024]{1,0:T(8,128)S(1)} custom-call(bf16[160,256]{1,0:T(8,128)(2,1)S(1)} %get-tuple-element.75.after.rest_0_, bf16[1024,256]{1,0:T(8,128)(2,1)S(1)} %get-tuple-element.66.q, bf16[256,1024]{1,0:T(8,128)(2,1)S(1)} %get-tuple-element.45.kt, bf16[1024,1024]{1,0:T(8,128)(2,1)S(1)} %get-tuple-element.67.v), custom_call_target="tpu_custom_call" | custom-call | tf_op jit(solution)/shard_map/inside/pallas_call | solution.py:378
  45.2 0.0 collective-permute-done.7.rest_1_
  45.2 0.0 collective-permute-done.8.rest_2_
  45.2 0.0 collective-permute-done.9.rest_3_
  45.2 4.7 %away.1.after = bf16[512,2048]{1,0:T(8,128)(2,1)S(1)} custom-call(f32[1024,1024]{1,0:T(8,128)S(1)} %inside.1.after.att, bf16[1024,256]{1,0:T(8,128)(2,1)S(1)} %get-tuple-element.66.q, f32[1024,1024]{1,0:T(8,128)S(1)} %inside.1.after.att, bf16[4,4,160,256]{3,2,1,0:T(8,128)(2,1)S(1)} %get-tuple-element.69.before, ...), custom_call_target="tpu_custom_call" | custom-call | tf_op jit(solution)/shard_map/away/pallas_call | solution.py:470
  49.9 3.5 %collective-permute-start.10 = (bf16[512,2048]{1,0:T(8,128)(2,1)S(1)}, bf16[512,2048]{1,0:T(8,128)(2,1)S(1)}, u32[]{:S(2)}, u32[]{:S(2)}) collective-permute-start(bf16[512,2048]{1,0:T(8,128)(2,1)S(1)} %away.1.after), channel_id=1, source_target_pairs={{0,1},{1,0},{2,3},{3,2},{4,5},{5,4},{6,7},{7,6},{8,9},{9,8},{10,11... | collective-permute-start | bytes 6291464 | tf_op jit(solution)/shard_map/ppermute | solution.py:538
  53.4 4.7 %home.1.own = bf16[512,2048]{1,0:T(8,128)(2,1)S(1)} custom-call(bf16[512,2048]{1,0:T(8,128)(2,1)S(1)} %away.1.after, bf16[1024,256]{1,0:T(8,128)(2,1)S(1)} %get-tuple-element.66.q, f32[1024,1024]{1,0:T(8,128)S(1)} %inside.1.after.att, bf16[4,4,160,256]{3,2,1,0:T(8,128)(2,1)S(1)} %get-tuple-element.69.before, bf16[1024,1024]{1,0:T(8,128)(2,1)S(1)} %get-tuple-element.70.gate, ...), custom_call_target="tpu_custom_call" | custom-call | tf_op jit(solution)/shard_map/home/pallas_call | solution.py:470
  58.1 0.0 collective-permute-done.10.other
  58.1 1.4 %join.1 = bf16[512,2048]{1,0:T(8,128)(2,1)} custom-call(bf16[512,2048]{1,0:T(8,128)(2,1)S(1)} %home.1.own, bf16[512,2048]{1,0:T(8,128)(2,1)S(1)} %collective-permute-done.10.other), custom_call_target="tpu_custom_call" | custom-call | tf_op jit(solution)/shard_map/join/pallas_call | solution.py:494
  (1 shorter events, 0.0 us)
Async XLA Ops:
  0.8 9.0 %collective-permute-start = (bf16[8,2048]{1,0:T(8,128)(2,1)S(1)}, bf16[8,2048]{1,0:T(8,128)(2,1)S(1)}, u32[]{:S(2)}, u32[]{:S(2)}) collective-permute-start(bf16[8,2048]{1,0:T(8,128)(2,1)S(1)} %slice.3), channel_id=1, source_target_pairs={{0,2},{2,4},{4,6},{6,8},{8,10},{10,12},{12,14},{14,16},{16,18},{18... | collective-permute-start | bytes 98312 | tf_op jit(solution)/shard_map/ppermute | solution.py:506
  17.8 9.3 %collective-permute-start.1 = (bf16[160,256]{1,0:T(8,128)(2,1)S(1)}, bf16[160,256]{1,0:T(8,128)(2,1)S(1)}, u32[]{:S(2)}, u32[]{:S(2)}) collective-permute-start(bf16[160,256]{1,0:T(8,128)(2,1)S(1)} %get-tuple-element.47), channel_id=1, source_target_pairs={{0,2},{2,4},{4,6},{6,0},{1,3},{3,5},{5,7},{7,1},{8,10},{10,12},{12... | collective-permute-start | bytes 245768 | tf_op jit(solution)/shard_map/ppermute | solution.py:510
  19.1 8.1 %collective-permute-start.2 = (bf16[160,256]{1,0:T(8,128)(2,1)S(1)}, bf16[160,256]{1,0:T(8,128)(2,1)S(1)}, u32[]{:S(2)}, u32[]{:S(2)}) collective-permute-start(bf16[160,256]{1,0:T(8,128)(2,1)S(1)} %get-tuple-element.48), channel_id=1, source_target_pairs={{0,4},{2,6},{4,0},{6,2},{1,5},{3,7},{5,1},{7,3},{8,12},{10,14},{12... | collective-permute-start | bytes 245768 | tf_op jit(solution)/shard_map/ppermute | solution.py:510
  20.3 6.8 %collective-permute-start.3 = (bf16[160,256]{1,0:T(8,128)(2,1)S(1)}, bf16[160,256]{1,0:T(8,128)(2,1)S(1)}, u32[]{:S(2)}, u32[]{:S(2)}) collective-permute-start(bf16[160,256]{1,0:T(8,128)(2,1)S(1)} %get-tuple-element.49), channel_id=1, source_target_pairs={{0,6},{2,0},{4,2},{6,4},{1,7},{3,1},{5,3},{7,5},{8,14},{10,8},{12,... | collective-permute-start | bytes 245768 | tf_op jit(solution)/shard_map/ppermute | solution.py:510
  27.2 10.4 %collective-permute-start.4 = (bf16[160,256]{1,0:T(8,128)(2,1)S(1)}, bf16[160,256]{1,0:T(8,128)(2,1)S(1)}, u32[]{:S(2)}, u32[]{:S(2)}) collective-permute-start(bf16[160,256]{1,0:T(8,128)(2,1)S(1)} %add_up.1), channel_id=1, source_target_pairs={{0,8},{8,16},{16,24},{24,0},{1,9},{9,17},{17,25},{25,1},{2,10},{10... | collective-permute-start | bytes 245768 | tf_op jit(solution)/shard_map/ppermute | solution.py:510
  28.6 9.1 %collective-permute-start.5 = (bf16[160,256]{1,0:T(8,128)(2,1)S(1)}, bf16[160,256]{1,0:T(8,128)(2,1)S(1)}, u32[]{:S(2)}, u32[]{:S(2)}) collective-permute-start(bf16[160,256]{1,0:T(8,128)(2,1)S(1)} %add_up.1), channel_id=1, source_target_pairs={{0,16},{8,24},{16,0},{24,8},{1,17},{9,25},{17,1},{25,9},{2,18},{10... | collective-permute-start | bytes 245768 | tf_op jit(solution)/shard_map/ppermute | solution.py:510
  30.9 6.8 %collective-permute-start.6 = (bf16[160,256]{1,0:T(8,128)(2,1)S(1)}, bf16[160,256]{1,0:T(8,128)(2,1)S(1)}, u32[]{:S(2)}, u32[]{:S(2)}) collective-permute-start(bf16[160,256]{1,0:T(8,128)(2,1)S(1)} %add_up.1), channel_id=1, source_target_pairs={{0,24},{8,0},{16,8},{24,16},{1,25},{9,1},{17,9},{25,17},{2,26},{10... | collective-permute-start | bytes 245768 | tf_op jit(solution)/shard_map/ppermute | solution.py:510
  37.9 7.3 %collective-permute-start.7 = (bf16[160,256]{1,0:T(8,128)(2,1)S(1)}, bf16[160,256]{1,0:T(8,128)(2,1)S(1)}, u32[]{:S(2)}, u32[]{:S(2)}) collective-permute-start(bf16[160,256]{1,0:T(8,128)(2,1)S(1)} %get-tuple-element.63), channel_id=1, source_target_pairs={{0,2},{2,4},{4,6},{6,0},{1,3},{3,5},{5,7},{7,1},{8,10},{10,12},{12... | collective-permute-start | bytes 245768 | tf_op jit(solution)/shard_map/ppermute | solution.py:510
  38.3 6.9 %collective-permute-start.8 = (bf16[160,256]{1,0:T(8,128)(2,1)S(1)}, bf16[160,256]{1,0:T(8,128)(2,1)S(1)}, u32[]{:S(2)}, u32[]{:S(2)}) collective-permute-start(bf16[160,256]{1,0:T(8,128)(2,1)S(1)} %get-tuple-element.64), channel_id=1, source_target_pairs={{0,4},{2,6},{4,0},{6,2},{1,5},{3,7},{5,1},{7,3},{8,12},{10,14},{12... | collective-permute-start | bytes 245768 | tf_op jit(solution)/shard_map/ppermute | solution.py:510
  38.5 6.7 %collective-permute-start.9 = (bf16[160,256]{1,0:T(8,128)(2,1)S(1)}, bf16[160,256]{1,0:T(8,128)(2,1)S(1)}, u32[]{:S(2)}, u32[]{:S(2)}) collective-permute-start(bf16[160,256]{1,0:T(8,128)(2,1)S(1)} %get-tuple-element.65), channel_id=1, source_target_pairs={{0,6},{2,0},{4,2},{6,4},{1,7},{3,1},{5,3},{7,5},{8,14},{10,8},{12,... | collective-permute-start | bytes 245768 | tf_op jit(solution)/shard_map/ppermute | solution.py:510
  49.9 8.2 %collective-permute-start.10 = (bf16[512,2048]{1,0:T(8,128)(2,1)S(1)}, bf16[512,2048]{1,0:T(8,128)(2,1)S(1)}, u32[]{:S(2)}, u32[]{:S(2)}) collective-permute-start(bf16[512,2048]{1,0:T(8,128)(2,1)S(1)} %away.1.after), channel_id=1, source_target_pairs={{0,1},{1,0},{2,3},{3,2},{4,5},{5,4},{6,7},{7,6},{8,9},{9,8},{10,11... | collective-permute-start | bytes 6291464 | tf_op jit(solution)/shard_map/ppermute | solution.py:538
